TPU v7x, 32 devices: a whole 2x2x4 slice. The times are simulated.
32 devices in a mesh: clip: 2 (over y), tile: 4 (over z), frame: 2 (over x), chan: 2 (over core).
Axes of the slice: x: 2, y: 2, z: 4, core: 2. Of those that a mesh axis runs over, the one named last changes fastest.
Arguments:
- features: bfloat16 [4, 8, 256, 256], P(('clip', 'frame'), 'tile', None, 'chan'), parts along dimension 0, may hold values from -6 to 6
- neighbours: int32 [16, 9], P(('clip', 'tile')), parts along dimension 0, may hold values from 0 to 7, as said below
- pairing: int32 [4, 2], P(('clip', 'frame')), parts along dimension 0, may hold values 0 or 1
- valid_tiles: int32 [16, 256], P(('clip', 'tile')), parts along dimension 0, may hold values 0 or 1
- cotangent: bfloat16 [4, 8, 256, 3060], P(('clip', 'frame'), 'tile', 'chan'), parts along dimension 0, may hold values from -6 to 6
Outputs:
- volume: bfloat16 [4, 8, 256, 3060], P(('clip', 'frame'), 'tile', 'chan'), parts along dimension 0
- feature_grad: float32 [4, 8, 256, 256], P(('clip', 'frame'), 'tile', None, 'chan'), parts along dimension 0
There are 2 independent parts, one for each index of `clip`. A program takes and returns all parts, laid end to end along the dimension named above; each array names one. Nothing has to cross between parts.
Inputs may be any that keep to these rules, and one draw needn't show every extreme that they name: `neighbours`: every entry of row a lies within 2 tiles of a, and in every row one entry lies exactly 2 tiles from a.
All inputs are finite; a program needn't handle non-finite values. No bound on the sum of `pairing` or of `valid_tiles` on one device may be relied on, other than what follows from the above.
Results may differ from a plain program's by a relative error of at most 0.008.
Values may be sent and summed in bfloat16 or wider, within the bound.
A program may use at most 64 MiB of HBM per device.

v0:
```python
import math

import jax
import jax.numpy as jnp
from jax import lax
from jax.sharding import PartitionSpec as P

CHANNELS = 256
SIDE = 16
PIXELS = 256
LEVELS = 340
NEIGHBOURS = 9


def with_halo(cells, sides, width):
    for axis, dim in sides:
        count = lax.axis_size(axis)
        ends = count - 1
        head = lax.slice_in_dim(cells, 0, width, axis=dim)
        tail = lax.slice_in_dim(cells, cells.shape[dim] - width, cells.shape[dim], axis=dim)
        cells = jnp.concatenate(
            [
                lax.ppermute(tail, axis, [(i, (i + 1) % count) for i in range(ends)]),
                cells,
                lax.ppermute(head, axis, [((i + 1) % count, i) for i in range(ends)]),
            ],
            axis=dim,
        )
    return cells


def pool_weights_table():
    pixel_ids = jnp.arange(PIXELS, dtype=jnp.int32)
    row_of = pixel_ids // SIDE
    column = pixel_ids % SIDE
    pieces = []
    for extent in (1, 2, 4, 8):
        across = SIDE // extent
        target = row_of // extent * across + column // extent
        member = jnp.arange(across * across, dtype=jnp.int32)[:, None] == target[None, :]
        pieces.append(member.astype(jnp.float32) / (extent * extent))
    return jnp.concatenate(pieces, 0)


def local(features, neighbours, pairing, valid_tiles, cotangent):
    tile_count = features.shape[1]
    half_rows = cotangent.shape[2]
    pool_weights = pool_weights_table()
    present = lax.all_gather(features, "chan", axis=3, tiled=True)
    framed = with_halo(present, (("frame", 0),), 1)
    partners = jnp.stack([framed[0], framed[2]], 0)
    window = with_halo(partners, (("tile", 1),), tile_count)
    pyramid = jnp.einsum(
        "mp,jwpc->jwmc",
        pool_weights.astype(jnp.bfloat16),
        window,
        preferred_element_type=jnp.float32,
    ).astype(jnp.bfloat16)
    core_index = lax.axis_index("chan")
    queries = lax.dynamic_slice_in_dim(present[0], core_index * half_rows, half_rows, 1)
    valid_local = lax.dynamic_slice_in_dim(valid_tiles, core_index * half_rows, half_rows, 1)
    slot_ids = neighbours - (lax.axis_index("tile") * tile_count - tile_count)
    chosen = pyramid[:, slot_ids]
    gates = pairing[0].astype(jnp.float32) / math.sqrt(CHANNELS)
    scores = jnp.einsum("apc,jakmc->japkm", queries, chosen, preferred_element_type=jnp.float32)
    summed = (
        jnp.sum(gates[:, None, None, None, None] * scores, axis=0)
        * valid_local.astype(jnp.float32)[:, :, None, None]
    )
    volume = summed.reshape(tile_count, half_rows, NEIGHBOURS * LEVELS).astype(jnp.bfloat16)[None]
    upstream = cotangent[0].reshape(tile_count, half_rows, NEIGHBOURS, LEVELS)
    upstream = upstream * valid_local.astype(jnp.bfloat16)[:, :, None, None]
    partial_query = jnp.einsum(
        "apkm,jakmc->japc", upstream, chosen, preferred_element_type=jnp.float32
    )
    query_grad = jnp.sum(gates[:, None, None, None] * partial_query, axis=0)
    base_grad = jnp.einsum("apkm,apc->akmc", upstream, queries, preferred_element_type=jnp.float32)
    member = (
        slot_ids[:, :, None] == jnp.arange(3 * tile_count, dtype=jnp.int32)[None, None, :]
    ).astype(jnp.float32)
    weighted_member = gates[:, None, None, None] * member[None]
    window_grad = jnp.einsum(
        "akmc,jakw->jwmc", base_grad, weighted_member, precision=lax.Precision.HIGHEST
    )
    window_grad = jnp.einsum(
        "mp,jwmc->jwpc", pool_weights, window_grad, precision=lax.Precision.HIGHEST
    )
    spread = with_halo(window_grad.astype(jnp.bfloat16), (("tile", 1),), tile_count).astype(
        window_grad.dtype
    )
    returned = (
        spread[:, :tile_count]
        + spread[:, 2 * tile_count : 3 * tile_count]
        + spread[:, 4 * tile_count :]
    )
    framed_back = with_halo(returned.astype(jnp.bfloat16), (("frame", 0),), 1).astype(
        returned.dtype
    )
    key_grad = framed_back[0] + framed_back[3]
    placed = lax.dynamic_update_slice_in_dim(
        jnp.zeros(key_grad.shape, jnp.float32), query_grad, core_index * half_rows, 1
    )
    feature_grad = lax.psum_scatter(key_grad + placed, "chan", scatter_dimension=2, tiled=True)
    return (volume, feature_grad[None])


def solution(mesh):
    return jax.shard_map(
        local,
        mesh=mesh,
        in_specs=(
            P(("clip", "frame"), "tile", None, "chan"),
            P(("clip", "tile"), None),
            P(("clip", "frame"), None),
            P(("clip", "tile"), None),
            P(("clip", "frame"), "tile", "chan", None),
        ),
        out_specs=(
            P(("clip", "frame"), "tile", "chan", None),
            P(("clip", "frame"), "tile", None, "chan"),
        ),
        check_vma=False,
    )
```

profile of v0, /device:TPU:0, one launch (start us, length us, event | category | flops | bytes accessed | tf_op | source)
XLA Modules:
  0.0 115.8 jit_solution(81603316902151556)
XLA Ops:
  7.2 0.0 reduce-scatter.2.cloned.1.call-start
  7.2 2.4 %all_gather.3 = bf16[1,2,256,256]{3,2,1,0:T(8,128)(2,1)S(1)} all-gather(bf16[1,2,256,128]{3,2,1,0:T(8,128)(2,1)} %param.5), channel_id=1, replica_groups=mesh['clip'=2,'tile'=4,'frame'=2,'chan'=2] {'chan'}, dimensions={3}, use_global_device_ids=true | all-gather | bytes 393216 | tf_op jit(solution)/shard_map/all_gather | solution.py:49
  9.6 0.0 copy-start.1
  9.6 0.7 compare_select_fusion
  10.3 0.7 multiply_bitcast_fusion
  11.0 0.7 fusion.73
  11.7 2.4 %fusion.38 = f32[2,9,340,256]{3,2,1,0:T(8,128)S(1)} fusion(bf16[2,128,9,340]{1,0,3,2:T(2,128)(2,1)} %bitcast.89, bf16[2,128]{1,0:T(2,128)(2,1)S(1)} %get-tuple-element.14, bf16[1,2,256,256]{3,2,1,0:T(8,128)(2,1)S(1)} %all_gather.3, s32[]{:T(128)S(6)} %select_n.113), kind=kOutput, calls=%fused_computation.27 | convolution fusion | flops 401863680 | bytes 7965188 | tf_op jit(solution)/shard_map/apkm,apc->akmc/dot_general | solution.py:77
  14.1 11.3 %fusion.11 = f32[2,6,340,256]{3,1,2,0:T(8,128)S(1)} fusion(f32[2,9,340,256]{3,2,1,0:T(8,128)S(1)} %fusion.38, f32[2,9,6]{1,2,0:T(8,128)S(1)} %fusion.64, f32[2]{0:T(128)S(1)} %multiply_bitcast_fusion), kind=kOutput, calls=%fused_computation.14 | convolution fusion | flops 225607904 | bytes 10445240 | tf_op jit(solution)/shard_map/akmc,jakw->jwmc/dot_general | solution.py:82
  25.5 8.4 %fusion.25 = bf16[2,6,256,256]{2,3,1,0:T(8,128)(2,1)S(1)} fusion(f32[2,6,340,256]{3,1,2,0:T(8,128)S(1)} %fusion.11, f32[4,256]{1,0:T(4,128)S(1)} %fusion.65, f32[16,256]{1,0:T(8,128)S(1)} %fusion.61, f32[64,256]{1,0:T(8,128)S(1)} %fusion.58, f32[256,256]{1,0:T(8,128)S(1)} %fusion.50), kind=kOutput, calls=%fused_computation.24 | convolution fusion | flops 3209690112 | bytes 6098944 | tf_op jit(solution)/shard_map/mp,jwmc->jwpc/dot_general | solution.py:85
  33.8 0.1 fusion.78
  33.9 4.9 %collective-permute-start.4 = (bf16[2,2,256,256]{2,3,1,0:T(8,128)(2,1)S(1)}, bf16[2,2,256,256]{2,3,1,0:T(8,128)(2,1)S(1)}, u32[]{:S(2)}, u32[]{:S(2)}) collective-permute-start(bf16[2,2,256,256]{2,3,1,0:T(8,128)(2,1)S(1)} %get-tuple-element.10), channel_id=1, source_target_pairs={{0,4},{4,8},{8,12},{1,5},{5,9},{9,13},{2,6},{6,10},{10,14},{3,7},{... | collective-permute-start | bytes 1572872 | tf_op jit(solution)/shard_map/ppermute | solution.py:23
  38.8 1.3 %collective-permute-start.5 = (bf16[2,2,256,256]{2,3,1,0:T(8,128)(2,1)S(1)}, bf16[2,2,256,256]{2,3,1,0:T(8,128)(2,1)S(1)}, u32[]{:S(2)}, u32[]{:S(2)}) collective-permute-start(bf16[2,2,256,256]{2,3,1,0:T(8,128)(2,1)S(1)} %get-tuple-element.11), channel_id=1, source_target_pairs={{4,0},{8,4},{12,8},{5,1},{9,5},{13,9},{6,2},{10,6},{14,10},{7,3},{... | collective-permute-start | bytes 1572872 | tf_op jit(solution)/shard_map/ppermute | solution.py:25
  40.1 3.4 %collective-permute-start = (bf16[1,2,256,256]{3,2,1,0:T(8,128)(2,1)S(1)}, bf16[1,2,256,256]{3,2,1,0:T(8,128)(2,1)S(1)}, u32[]{:S(2)}, u32[]{:S(2)}) collective-permute-start(bf16[1,2,256,256]{3,2,1,0:T(8,128)(2,1)S(1)} %all_gather.3), channel_id=1, source_target_pairs={{0,2},{1,3},{4,6},{5,7},{8,10},{9,11},{12,14},{13,15},{16,18},{17,... | collective-permute-start | bytes 786440 | tf_op jit(solution)/shard_map/ppermute | solution.py:23
  43.5 0.0 copy-done.1
  43.5 1.3 %collective-permute-start.1 = (bf16[1,2,256,256]{3,2,1,0:T(8,128)(2,1)S(1)}, bf16[1,2,256,256]{3,2,1,0:T(8,128)(2,1)S(1)}, u32[]{:S(2)}, u32[]{:S(2)}) collective-permute-start(bf16[1,2,256,256]{3,2,1,0:T(8,128)(2,1)S(1)} %all_gather.3), channel_id=1, source_target_pairs={{2,0},{3,1},{6,4},{7,5},{10,8},{11,9},{14,12},{15,13},{18,16},{19,... | collective-permute-start | bytes 786440 | tf_op jit(solution)/shard_map/ppermute | solution.py:25
  44.8 4.2 %collective-permute-done = bf16[1,2,256,256]{3,2,1,0:T(8,128)(2,1)S(1)} collective-permute-done((bf16[1,2,256,256]{3,2,1,0:T(8,128)(2,1)S(1)}, bf16[1,2,256,256]{3,2,1,0:T(8,128)(2,1)S(1)}, u32[]{:S(2)}, u32[]{:S(2)}) %collective-permute-start) | collective-permute-done | bytes 262176 | tf_op jit(solution)/shard_map/ppermute | solution.py:23
  49.1 0.7 constant_dynamic-update-slice_fusion.1
  49.8 3.4 %collective-permute-done.1 = bf16[1,2,256,256]{3,2,1,0:T(8,128)(2,1)S(1)} collective-permute-done((bf16[1,2,256,256]{3,2,1,0:T(8,128)(2,1)S(1)}, bf16[1,2,256,256]{3,2,1,0:T(8,128)(2,1)S(1)}, u32[]{:S(2)}, u32[]{:S(2)}) %collective-permute-start.1) | collective-permute-done | bytes 262176 | tf_op jit(solution)/shard_map/ppermute | solution.py:25
  53.2 0.7 constant_dynamic-update-slice_fusion
  53.9 4.3 %collective-permute-start.2 = (bf16[2,2,256,256]{3,2,1,0:T(8,128)(2,1)}, bf16[2,2,256,256]{3,2,1,0:T(8,128)(2,1)S(1)}, u32[]{:S(2)}, u32[]{:S(2)}) collective-permute-start(bf16[2,2,256,256]{3,2,1,0:T(8,128)(2,1)} %constant_dynamic-update-slice_fusion), channel_id=1, source_target_pairs={{0,4},{4,8},{8,12},{1,5},{5,9},{9,13},{2,6},{6,10},{10,14},{3,7},{... | collective-permute-start | bytes 1572872 | tf_op jit(solution)/shard_map/ppermute | solution.py:23
  58.2 1.3 %collective-permute-start.3 = (bf16[2,2,256,256]{3,2,1,0:T(8,128)(2,1)}, bf16[2,2,256,256]{3,2,1,0:T(8,128)(2,1)}, u32[]{:S(2)}, u32[]{:S(2)}) collective-permute-start(bf16[2,2,256,256]{3,2,1,0:T(8,128)(2,1)} %constant_dynamic-update-slice_fusion), channel_id=1, source_target_pairs={{4,0},{8,4},{12,8},{5,1},{9,5},{13,9},{6,2},{10,6},{14,10},{7,3},{... | collective-permute-start | bytes 1572872 | tf_op jit(solution)/shard_map/ppermute | solution.py:25
  59.5 0.0 collective-permute-done.4
  59.5 0.0 collective-permute-done.5
  59.5 0.3 fusion.45
  59.9 1.5 %collective-permute-start.6 = (bf16[1,2,256,256]{2,3,1,0:T(8,128)(2,1)S(1)}, bf16[1,2,256,256]{2,3,1,0:T(8,128)(2,1)S(1)}, u32[]{:S(2)}, u32[]{:S(2)}) collective-permute-start(bf16[1,2,256,256]{2,3,1,0:T(8,128)(2,1)S(1)} %get-tuple-element.12), channel_id=1, source_target_pairs={{0,2},{1,3},{4,6},{5,7},{8,10},{9,11},{12,14},{13,15},{16,18},{17,... | collective-permute-start | bytes 786440 | tf_op jit(solution)/shard_map/ppermute | solution.py:23
  61.3 1.5 %collective-permute-start.7 = (bf16[1,2,256,256]{2,3,1,0:T(8,128)(2,1)S(1)}, bf16[1,2,256,256]{2,3,1,0:T(8,128)(2,1)S(1)}, u32[]{:S(2)}, u32[]{:S(2)}) collective-permute-start(bf16[1,2,256,256]{2,3,1,0:T(8,128)(2,1)S(1)} %get-tuple-element.13), channel_id=1, source_target_pairs={{2,0},{3,1},{6,4},{7,5},{10,8},{11,9},{14,12},{15,13},{18,16},{19,... | collective-permute-start | bytes 786440 | tf_op jit(solution)/shard_map/ppermute | solution.py:25
  62.8 0.1 reshape.150
  62.9 2.4 %collective-permute-done.6 = bf16[1,2,256,256]{2,3,1,0:T(8,128)(2,1)S(1)} collective-permute-done((bf16[1,2,256,256]{2,3,1,0:T(8,128)(2,1)S(1)}, bf16[1,2,256,256]{2,3,1,0:T(8,128)(2,1)S(1)}, u32[]{:S(2)}, u32[]{:S(2)}) %collective-permute-start.6) | collective-permute-done | bytes 262176 | tf_op jit(solution)/shard_map/ppermute | solution.py:23
  65.3 4.3 %collective-permute-done.7 = bf16[1,2,256,256]{2,3,1,0:T(8,128)(2,1)S(1)} collective-permute-done((bf16[1,2,256,256]{2,3,1,0:T(8,128)(2,1)S(1)}, bf16[1,2,256,256]{2,3,1,0:T(8,128)(2,1)S(1)}, u32[]{:S(2)}, u32[]{:S(2)}) %collective-permute-start.7) | collective-permute-done | bytes 262176 | tf_op jit(solution)/shard_map/ppermute | solution.py:25
  69.6 0.1 convert_add_fusion.1
  69.7 0.0 collective-permute-done.2
  69.7 0.0 copy-start.3
  69.7 0.8 copy-done.3
  70.5 1.9 %collective-permute-done.3 = bf16[2,2,256,256]{3,2,1,0:T(8,128)(2,1)} collective-permute-done((bf16[2,2,256,256]{3,2,1,0:T(8,128)(2,1)}, bf16[2,2,256,256]{3,2,1,0:T(8,128)(2,1)}, u32[]{:S(2)}, u32[]{:S(2)}) %collective-permute-start.3) | collective-permute-done | bytes 524320 | tf_op jit(solution)/shard_map/ppermute | solution.py:25
  72.4 2.1 %convert_bitcast_fusion = bf16[2,6,340,256]{3,2,1,0:T(8,128)(2,1)S(1)} fusion(bf16[2,2,256,256]{3,2,1,0:T(8,128)(2,1)} %collective-permute-done.3, bf16[2,2,256,256]{3,2,1,0:T(8,128)(2,1)} %constant_dynamic-update-slice_fusion, bf16[2,2,256,256]{3,2,1,0:T(8,128)(2,1)} %copy-done.3, f32[4,256]{1,0:T(4,128)S(1)} %fusion.65, f32[16,256]{1,0:T(8,128)S(1)} %fusion.61, ...), kind=kOutput, calls=%fused_computation.15 | convolution fusion | flops 538087424 | bytes 4009984 | tf_op jit(solution)/shard_map/mp,jwpc->jwmc/dot_general | solution.py:53
  74.6 4.7 %gather_fusion = bf16[18,2,340,256]{3,2,1,0:T(8,128)(2,1)} fusion(bf16[2,6,340,256]{3,2,1,0:T(8,128)(2,1)S(1)} %convert_bitcast_fusion, s32[1024]{0:T(1024)S(1)} %pad_clamp_fusion), kind=kCustom, calls=%fused_computation | custom fusion | bytes 12533832 | tf_op jit(solution)/shard_map/gather | solution.py:63
  79.3 0.0 copy-start.2
  79.3 6.0 %fusion.39 = f32[2,256,128]{2,1,0:T(8,128)S(1)} fusion(bf16[2,128,9,340]{1,0,3,2:T(2,128)(2,1)} %bitcast.90, bf16[2,9,2,340,256]{4,3,2,1,0:T(8,128)(2,1)} %bitcast.85, bf16[2,128]{1,0:T(2,128)(2,1)S(1)} %get-tuple-element.14, f32[2]{0:T(128)S(1)} %multiply_bitcast_fusion), kind=kOutput, calls=%fused_computation.28 | convolution fusion | flops 803140608 | bytes 8096264 | tf_op jit(solution)/shard_map/apkm,jakmc->japc/dot_general | solution.py:73
  85.3 0.0 copy-start
  85.3 0.8 copy-done
  86.1 0.0 reduce-scatter.2.cloned.1.call-update
  86.1 0.0 copy-done.2
  86.2 6.6 %multiply_reduce_fusion = f32[2,9,340,128]{3,2,1,0:T(8,128)} fusion(f32[2]{0:T(128)S(1)} %multiply_bitcast_fusion, bf16[2,9,2,340,256]{4,3,2,1,0:T(8,128)(2,1)} %bitcast.86, bf16[1,2,256,256]{3,2,1,0:T(8,128)(2,1)S(1)} %copy-done.2, s32[]{:T(128)S(6)} %select_n.113), kind=kOutput, calls=%fused_computation.8 | convolution fusion | flops 804510720 | bytes 9531908 | tf_op jit(solution)/shard_map/apc,jakmc->japkm/dot_general | solution.py:65
  92.7 2.1 %reduce_sum.26 = f32[1,2,128,3060]{2,3,1,0:T(8,128)S(1)} reshape(f32[2,128,9,340]{1,3,2,0:T(8,128)} %bitcast.88) | data formatting | bytes 6266880 | tf_op jit(solution)/shard_map/reduce_sum | solution.py:67
  94.8 0.2 multiply_convert_fusion
  95.0 12.1 %copy.18 = bf16[1,2,128,3060]{2,1,3,0:T(2,128)(2,1)} copy(bf16[1,2,128,3060]{2,3,1,0:T(8,128)(2,1)S(1)} %multiply_convert_fusion) | data formatting | bytes 3133440
  107.2 0.0 reduce-scatter.2.cloned.1.call-done
  107.2 1.8 %copy.19 = f32[1,2,256,128]{3,2,1,0:T(8,128)} copy(f32[1,2,256,128]{2,3,1,0:T(8,128)} %bitcast.91) | data formatting | bytes 524288
  (11 shorter events, 0.2 us)
Async XLA Ops:
  7.2 100.0 %reduce-scatter.2.cloned.1.call-start = ((), (), s32[]{:S(2)}) async-start(), calls=%async_computation.1 | async-start | bytes 786432 | tf_op jit(solution)/shard_map/reduce_scatter | solution.py:103
  9.6 33.9 %copy-start.1 = (bf16[1,2,256,256]{3,2,1,0:T(8,128)(2,1)}, bf16[1,2,256,256]{3,2,1,0:T(8,128)(2,1)S(1)}, u32[]{:S(2)}) copy-start(bf16[1,2,256,256]{3,2,1,0:T(8,128)(2,1)S(1)} %all_gather.3) | copy-start | bytes 786436
  33.9 25.6 %collective-permute-start.4 = (bf16[2,2,256,256]{2,3,1,0:T(8,128)(2,1)S(1)}, bf16[2,2,256,256]{2,3,1,0:T(8,128)(2,1)S(1)}, u32[]{:S(2)}, u32[]{:S(2)}) collective-permute-start(bf16[2,2,256,256]{2,3,1,0:T(8,128)(2,1)S(1)} %get-tuple-element.10), channel_id=1, source_target_pairs={{0,4},{4,8},{8,12},{1,5},{5,9},{9,13},{2,6},{6,10},{10,14},{3,7},{... | collective-permute-start | bytes 1572872 | tf_op jit(solution)/shard_map/ppermute | solution.py:23
  38.8 20.7 %collective-permute-start.5 = (bf16[2,2,256,256]{2,3,1,0:T(8,128)(2,1)S(1)}, bf16[2,2,256,256]{2,3,1,0:T(8,128)(2,1)S(1)}, u32[]{:S(2)}, u32[]{:S(2)}) collective-permute-start(bf16[2,2,256,256]{2,3,1,0:T(8,128)(2,1)S(1)} %get-tuple-element.11), channel_id=1, source_target_pairs={{4,0},{8,4},{12,8},{5,1},{9,5},{13,9},{6,2},{10,6},{14,10},{7,3},{... | collective-permute-start | bytes 1572872 | tf_op jit(solution)/shard_map/ppermute | solution.py:25
  40.1 9.0 %collective-permute-start = (bf16[1,2,256,256]{3,2,1,0:T(8,128)(2,1)S(1)}, bf16[1,2,256,256]{3,2,1,0:T(8,128)(2,1)S(1)}, u32[]{:S(2)}, u32[]{:S(2)}) collective-permute-start(bf16[1,2,256,256]{3,2,1,0:T(8,128)(2,1)S(1)} %all_gather.3), channel_id=1, source_target_pairs={{0,2},{1,3},{4,6},{5,7},{8,10},{9,11},{12,14},{13,15},{16,18},{17,... | collective-permute-start | bytes 786440 | tf_op jit(solution)/shard_map/ppermute | solution.py:23
  43.5 9.7 %collective-permute-start.1 = (bf16[1,2,256,256]{3,2,1,0:T(8,128)(2,1)S(1)}, bf16[1,2,256,256]{3,2,1,0:T(8,128)(2,1)S(1)}, u32[]{:S(2)}, u32[]{:S(2)}) collective-permute-start(bf16[1,2,256,256]{3,2,1,0:T(8,128)(2,1)S(1)} %all_gather.3), channel_id=1, source_target_pairs={{2,0},{3,1},{6,4},{7,5},{10,8},{11,9},{14,12},{15,13},{18,16},{19,... | collective-permute-start | bytes 786440 | tf_op jit(solution)/shard_map/ppermute | solution.py:25
  53.9 15.8 %collective-permute-start.2 = (bf16[2,2,256,256]{3,2,1,0:T(8,128)(2,1)}, bf16[2,2,256,256]{3,2,1,0:T(8,128)(2,1)S(1)}, u32[]{:S(2)}, u32[]{:S(2)}) collective-permute-start(bf16[2,2,256,256]{3,2,1,0:T(8,128)(2,1)} %constant_dynamic-update-slice_fusion), channel_id=1, source_target_pairs={{0,4},{4,8},{8,12},{1,5},{5,9},{9,13},{2,6},{6,10},{10,14},{3,7},{... | collective-permute-start | bytes 1572872 | tf_op jit(solution)/shard_map/ppermute | solution.py:23
  58.2 14.2 %collective-permute-start.3 = (bf16[2,2,256,256]{3,2,1,0:T(8,128)(2,1)}, bf16[2,2,256,256]{3,2,1,0:T(8,128)(2,1)}, u32[]{:S(2)}, u32[]{:S(2)}) collective-permute-start(bf16[2,2,256,256]{3,2,1,0:T(8,128)(2,1)} %constant_dynamic-update-slice_fusion), channel_id=1, source_target_pairs={{4,0},{8,4},{12,8},{5,1},{9,5},{13,9},{6,2},{10,6},{14,10},{7,3},{... | collective-permute-start | bytes 1572872 | tf_op jit(solution)/shard_map/ppermute | solution.py:25
  59.9 5.5 %collective-permute-start.6 = (bf16[1,2,256,256]{2,3,1,0:T(8,128)(2,1)S(1)}, bf16[1,2,256,256]{2,3,1,0:T(8,128)(2,1)S(1)}, u32[]{:S(2)}, u32[]{:S(2)}) collective-permute-start(bf16[1,2,256,256]{2,3,1,0:T(8,128)(2,1)S(1)} %get-tuple-element.12), channel_id=1, source_target_pairs={{0,2},{1,3},{4,6},{5,7},{8,10},{9,11},{12,14},{13,15},{16,18},{17,... | collective-permute-start | bytes 786440 | tf_op jit(solution)/shard_map/ppermute | solution.py:23
  61.3 8.3 %collective-permute-start.7 = (bf16[1,2,256,256]{2,3,1,0:T(8,128)(2,1)S(1)}, bf16[1,2,256,256]{2,3,1,0:T(8,128)(2,1)S(1)}, u32[]{:S(2)}, u32[]{:S(2)}) collective-permute-start(bf16[1,2,256,256]{2,3,1,0:T(8,128)(2,1)S(1)} %get-tuple-element.13), channel_id=1, source_target_pairs={{2,0},{3,1},{6,4},{7,5},{10,8},{11,9},{14,12},{15,13},{18,16},{19,... | collective-permute-start | bytes 786440 | tf_op jit(solution)/shard_map/ppermute | solution.py:25
  69.7 0.8 copy-start.3
  79.3 6.9 %copy-start.2 = (bf16[1,2,256,256]{3,2,1,0:T(8,128)(2,1)S(1)}, bf16[1,2,256,256]{3,2,1,0:T(8,128)(2,1)}, u32[]{:S(2)}) copy-start(bf16[1,2,256,256]{3,2,1,0:T(8,128)(2,1)} %copy-done.1) | copy-start | bytes 786436
  85.3 0.8 copy-start
Sparse Core Ops, SparseCore 0:
  86.3 8.2 reduce-scatter.1
where the time goes:
time: 116 us
  matrix products  36.8 us (32%)
  local copies, waits for them, and re-layouts  23.9 us (21%)
  starting transfers between devices  19.4 us (17%)
  waiting for transfers between devices  16.2 us (14%)
  between operations  14.3 us (12%)
  other arithmetic  2.76 us (2%)
  blocking collectives  2.36 us (2%)
    unnamed x12, local copies, waits for them, and re-layouts  16.3 us
    ppermute x4, starting transfers between devices, with_halo(): lax.ppermute(tail, axis, [(i, (i + 1) % count) for i in range(ends)])  14 us
    dot_general x1, matrix products, local(): jnp.einsum('akmc,jakw->jwmc', base_grad, weighted_member, precision=lax.P...  11.3 us
    ppermute x4, waiting for transfers between devices, with_halo(): lax.ppermute(head, axis, [((i + 1) % count, i) for i in range(ends)])  9.58 us
    dot_general x1, matrix products, local(): jnp.einsum('mp,jwmc->jwpc', pool_weights, window_grad, precision=lax.Prec...  8.35 us
    ppermute x4, waiting for transfers between devices, with_halo(): lax.ppermute(tail, axis, [(i, (i + 1) % count) for i in range(ends)])  6.63 us
    dot_general x1, matrix products, local(): jnp.einsum('apc,jakmc->japkm', queries, chosen, preferred_element_type=jn...  6.57 us
    dot_general x1, matrix products, local(): jnp.einsum('apkm,jakmc->japc', upstream, chosen, preferred_element_type=j...  5.99 us
  transfers between devices with their start and end apart: 9, of which 5 were waited for; matrix products, arithmetic and copies ran while one was open for 20% of the time, Pallas kernels for 0%

commit v1 on v0

v1 whole, which is shorter than its diff:
```python
import math

import jax
import jax.numpy as jnp
from jax import lax
from jax.sharding import PartitionSpec as P

CHANNELS = 256
SIDE = 16
PIXELS = 256
LEVELS = 340
NEIGHBOURS = 9
EXTENTS = (1, 2, 4, 8)


def shift(x, axis, step):
    count = lax.axis_size(axis)
    if step > 0:
        pairs = [(i, i + 1) for i in range(count - 1)]
    else:
        pairs = [(i + 1, i) for i in range(count - 1)]
    return lax.ppermute(x, axis, pairs)


def pool_weights_table():
    pixel_ids = jnp.arange(PIXELS, dtype=jnp.int32)
    row_of = pixel_ids // SIDE
    column = pixel_ids % SIDE
    pieces = []
    for extent in EXTENTS:
        across = SIDE // extent
        target = row_of // extent * across + column // extent
        member = jnp.arange(across * across, dtype=jnp.int32)[:, None] == target[None, :]
        pieces.append(member.astype(jnp.float32) / (extent * extent))
    return jnp.concatenate(pieces, 0)


def pool_back(cells):
    lead = cells.shape[0]
    chans = cells.shape[-1]
    total = None
    start = 0
    for extent in EXTENTS:
        across = SIDE // extent
        part = cells[:, start : start + across * across] * (1.0 / (extent * extent))
        start += across * across
        part = part.reshape(lead, across, 1, across, 1, chans)
        part = jnp.broadcast_to(part, (lead, across, extent, across, extent, chans))
        part = part.reshape(lead, PIXELS, chans)
        total = part if total is None else total + part
    return total


def local(features, neighbours, pairing, valid_tiles, cotangent):
    tile_count = features.shape[1]
    half_rows = cotangent.shape[2]
    pool_weights = pool_weights_table()
    present = lax.all_gather(features, "chan", axis=3, tiled=True)[0]
    before = shift(present, "frame", 1)
    after = shift(present, "frame", -1)
    partners = jnp.stack([before, after], 0)
    window = jnp.concatenate(
        [shift(partners, "tile", 1), partners, shift(partners, "tile", -1)], axis=1
    )
    pyramid = jnp.einsum(
        "mp,jwpc->jwmc",
        pool_weights.astype(jnp.bfloat16),
        window,
        preferred_element_type=jnp.float32,
    ).astype(jnp.bfloat16)
    gate01 = pairing[0].astype(jnp.bfloat16)
    pyramid = pyramid * gate01[:, None, None, None]
    core_index = lax.axis_index("chan")
    queries = lax.dynamic_slice_in_dim(present, core_index * half_rows, half_rows, 1)
    valid_local = lax.dynamic_slice_in_dim(valid_tiles, core_index * half_rows, half_rows, 1)
    scale = valid_local.astype(jnp.float32) * (1.0 / math.sqrt(CHANNELS))
    slot_ids = neighbours - (lax.axis_index("tile") * tile_count - tile_count)
    chosen = pyramid[:, slot_ids]
    queries2 = jnp.broadcast_to(queries[None], (2,) + queries.shape)
    scores = jnp.einsum(
        "jakmc,japc->kmap", chosen, queries2, preferred_element_type=jnp.float32
    )
    summed = scores * scale[None, None]
    volume = summed.reshape(NEIGHBOURS * LEVELS, tile_count, half_rows).astype(jnp.bfloat16)
    volume = jnp.transpose(volume, (1, 2, 0))[None]
    upstream = cotangent[0].reshape(tile_count, half_rows, NEIGHBOURS, LEVELS)
    upstream = upstream * valid_local.astype(jnp.bfloat16)[:, :, None, None]
    partial_query = jnp.einsum(
        "apkm,jakmc->japc", upstream, chosen, preferred_element_type=jnp.float32
    )
    query_grad = jnp.sum(partial_query, axis=0) * (1.0 / math.sqrt(CHANNELS))
    base_grad = jnp.einsum("apkm,apc->akmc", upstream, queries, preferred_element_type=jnp.float32)
    member = (
        slot_ids[:, :, None] == jnp.arange(3 * tile_count, dtype=jnp.int32)[None, None, :]
    ).astype(jnp.float32)
    cells = jnp.sum(member[:, :, :, None, None] * base_grad[:, :, None], axis=(0, 1))
    window_grad = pool_back(cells)
    sent_left = shift(window_grad[:tile_count].astype(jnp.bfloat16), "tile", -1)
    sent_right = shift(window_grad[2 * tile_count :].astype(jnp.bfloat16), "tile", 1)
    returned = (
        sent_left.astype(jnp.float32)
        + window_grad[tile_count : 2 * tile_count]
        + sent_right.astype(jnp.float32)
    )
    gates = pairing[0].astype(jnp.float32) * (1.0 / math.sqrt(CHANNELS))
    from_next = shift((returned * gates[0]).astype(jnp.bfloat16), "frame", -1)
    from_prev = shift((returned * gates[1]).astype(jnp.bfloat16), "frame", 1)
    key_grad = from_prev.astype(jnp.float32) + from_next.astype(jnp.float32)
    placed = lax.dynamic_update_slice_in_dim(
        jnp.zeros(key_grad.shape, jnp.float32), query_grad, core_index * half_rows, 1
    )
    feature_grad = lax.psum_scatter(key_grad + placed, "chan", scatter_dimension=2, tiled=True)
    return (volume, feature_grad[None])


def solution(mesh):
    return jax.shard_map(
        local,
        mesh=mesh,
        in_specs=(
            P(("clip", "frame"), "tile", None, "chan"),
            P(("clip", "tile"), None),
            P(("clip", "frame"), None),
            P(("clip", "tile"), None),
            P(("clip", "frame"), "tile", "chan", None),
        ),
        out_specs=(
            P(("clip", "frame"), "tile", "chan", None),
            P(("clip", "frame"), "tile", None, "chan"),
        ),
        check_vma=False,
    )
```

time: 116 us -> 218 us (1.88)
  other arithmetic: 2.76 us -> 120 us
  matrix products: 36.8 us -> 14.7 us
  local copies, waits for them, and re-layouts: 23.9 us -> 34.2 us
  waiting for transfers between devices: 16.2 us -> 7.07 us
  starting transfers between devices: 19.4 us -> 24.1 us
    reduce_sum x0 -> x1, other arithmetic: none -> 112 us  [local(): jnp.sum(member[:, :, :, None, None] * base_grad[:, :, None], axis=(0, 1))]
    dot_general x3 -> x1, matrix products: 26.3 us -> 4.64 us  [local(): jnp.einsum('jakmc,japc->kmap', chosen, queries2, preferred_element_type=j...]
    ppermute x8, waiting for transfers between devices: 16.2 us -> 7.05 us  [shift(): return lax.ppermute(x, axis, pairs)]
    reshape x0 -> x2, local copies, waits for them, and re-layouts: none -> 5.93 us  [pool_back(): part = part.reshape(lead, PIXELS, chans)]
    dot_general x0 -> x1, local copies, waits for them, and re-layouts: none -> 5.87 us  [local(): jnp.einsum('apkm,apc->akmc', upstream, queries, preferred_element_type=jn...]
    ppermute x8, starting transfers between devices: 19.4 us -> 24.1 us  [shift(): return lax.ppermute(x, axis, pairs)]
    another operation x0 -> x6, other arithmetic: none -> 4.51 us
    broadcast_in_dim x0 -> x5, local copies, waits for them, and re-layouts: none -> 3.54 us  [the longest x4 3.52 us: pool_back(): part = jnp.broadcast_to(part, (lead, across, extent, across, extent, chans))]
  transfers between devices with their start and end apart: 9 -> 9, of which waited for: 5 -> 2; matrix products, arithmetic and copies ran while one was open for 20% -> 72% of each run, Pallas kernels for 0% -> 0%
where the time goes in v1:
time: 218 us; the launch traced here: 217 us
  other arithmetic  120 us (55%)
  local copies, waits for them, and re-layouts  34.2 us (16%)
  starting transfers between devices  24.1 us (11%)
  matrix products  14.7 us (7%)
  between operations  14.4 us (7%)
  waiting for transfers between devices  7.07 us (3%)
  blocking collectives  2.36 us (1%)
    reduce_sum x1, other arithmetic, local(): jnp.sum(member[:, :, :, None, None] * base_grad[:, :, None], axis=(0, 1))  112 us
    ppermute x8, starting transfers between devices, shift(): return lax.ppermute(x, axis, pairs)  24.1 us
    unnamed x9, local copies, waits for them, and re-layouts  12.9 us
    ppermute x8, waiting for transfers between devices, shift(): return lax.ppermute(x, axis, pairs)  7.05 us
    reshape x2, local copies, waits for them, and re-layouts, pool_back(): part = part.reshape(lead, PIXELS, chans)  5.93 us
    dot_general x1, matrix products, local(): jnp.einsum('apkm,jakmc->japc', upstream, chosen, preferred_element_type=j...  5.91 us
    dot_general x1, local copies, waits for them, and re-layouts, local(): jnp.einsum('apkm,apc->akmc', upstream, queries, preferred_element_type=jn...  5.87 us
    gather x1, local copies, waits for them, and re-layouts, local(): chosen = pyramid[:, slot_ids]  4.68 us
  transfers between devices with their start and end apart: 9, of which 2 were waited for; matrix products, arithmetic and copies ran while one was open for 72% of the time, Pallas kernels for 0%

profile of v1, /device:TPU:0, one launch (start us, length us, event | category | flops | bytes accessed | tf_op | source)
XLA Modules:
  0.0 216.9 jit_solution(1151412918666723411)
XLA Ops:
  7.2 0.0 reduce-scatter.2.cloned.1.call-start
  7.2 2.4 %all_gather.3 = bf16[1,2,256,256]{3,2,1,0:T(8,128)(2,1)S(1)} all-gather(bf16[1,2,256,128]{3,2,1,0:T(8,128)(2,1)} %param.5), channel_id=1, replica_groups=mesh['clip'=2,'tile'=4,'frame'=2,'chan'=2] {'chan'}, dimensions={3}, use_global_device_ids=true | all-gather | bytes 393216 | tf_op jit(solution)/shard_map/all_gather | solution.py:58
  9.6 5.4 %collective-permute-start = (bf16[2,256,256]{2,1,0:T(8,128)(2,1)S(1)}, bf16[2,256,256]{2,1,0:T(8,128)(2,1)}, u32[]{:S(2)}, u32[]{:S(2)}) collective-permute-start(bf16[2,256,256]{2,1,0:T(8,128)(2,1)S(1)} %bitcast.79), channel_id=1, source_target_pairs={{0,2},{1,3},{4,6},{5,7},{8,10},{9,11},{12,14},{13,15},{16,18},{17,... | collective-permute-start | bytes 786440 | tf_op jit(solution)/shard_map/ppermute | solution.py:22
  15.0 1.3 collective-permute-start.1
  16.3 0.7 fusion.48
  17.0 2.4 %fusion.20 = f32[2,9,340,256]{3,2,1,0:T(8,128)S(1)} fusion(bf16[2,128,9,340]{1,0,3,2:T(2,128)(2,1)} %bitcast.77, bf16[2,128]{1,0:T(2,128)(2,1)S(1)} %fusion.48, bf16[1,2,256,256]{3,2,1,0:T(8,128)(2,1)S(1)} %all_gather.3, s32[]{:T(128)S(6)} %select_n.104), kind=kOutput, calls=%fused_computation.22 | convolution fusion | flops 401863680 | bytes 7965188 | tf_op jit(solution)/shard_map/apkm,apc->akmc/dot_general | solution.py:92
  19.4 0.0 copy-start.2
  19.4 5.9 %copy.35 = f32[2,9,340,256]{3,0,2,1:T(2,128)} copy(f32[2,9,340,256]{3,2,1,0:T(8,128)S(1)} %fusion.20) | data formatting | bytes 12533760 | tf_op jit(solution)/shard_map/apkm,apc->akmc/dot_general | solution.py:92
  25.3 0.0 copy-done.2
  25.3 0.1 copy.33
  25.4 112.2 %multiply_reduce_fusion = f32[6,340,256]{2,1,0:T(8,128)S(1)} fusion(f32[2,9,340,256]{3,0,2,1:T(2,128)} %copy.35, f32[2,9,6]{0,2,1:T(8,128)S(1)} %fusion.41), kind=kLoop, calls=%fused_computation.1 | loop fusion | flops 18278400 | bytes 8356272 | tf_op jit(solution)/shard_map/reduce_sum | solution.py:96
  137.7 1.9 broadcast_in_dim.27
  139.6 3.2 %reshape.148 = f32[6,256,256]{2,1,0:T(8,128)} reshape(f32[6,8,2,8,2,256]{5,4,3,2,1,0:T(2,128)} %broadcast_in_dim.27) | data formatting | bytes 3145728 | tf_op jit(solution)/shard_map/reshape | solution.py:49
  142.8 1.5 broadcast_in_dim.29
  144.4 2.8 %reshape.149 = f32[6,256,256]{2,1,0:T(8,128)} reshape(f32[6,4,4,4,4,256]{5,4,3,2,1,0:T(4,128)} %broadcast_in_dim.29) | data formatting | bytes 3145728 | tf_op jit(solution)/shard_map/reshape | solution.py:49
  147.2 0.0 copy-start.3
  147.2 3.4 %fusion.50 = (bf16[6,256,256]{2,1,0:T(8,128)(2,1)S(1)}, f32[6,256,256]{2,1,0:T(8,128)}) fusion(f32[6,2,2,256]{3,2,1,0:T(2,128)S(1)} %broadcast_in_dim.30, f32[6,256,256]{2,1,0:T(8,128)} %reshape.149, f32[6,256,256]{2,1,0:T(8,128)} %reshape.148, f32[6,340,256]{2,1,0:T(8,128)S(1)} %multiply_reduce_fusion), kind=kLoop, calls=%fused_computation.105 | loop fusion | flops 1572864 | bytes 7102464 | tf_op jit(solution)/shard_map/convert.1
  150.6 1.3 collective-permute-start.4
  151.9 4.6 %collective-permute-start.5 = (bf16[2,256,256]{2,1,0:T(8,128)(2,1)S(1)}, bf16[2,256,256]{2,1,0:T(8,128)(2,1)S(1)}, u32[]{:S(2)}, u32[]{:S(2)}) collective-permute-start(bf16[2,256,256]{2,1,0:T(8,128)(2,1)S(1)} %get-tuple-element.17), channel_id=1, source_target_pairs={{0,4},{4,8},{8,12},{1,5},{5,9},{9,13},{2,6},{6,10},{10,14},{3,7},{... | collective-permute-start | bytes 786440 | tf_op jit(solution)/shard_map/ppermute | solution.py:22
  156.6 0.1 reshape.153
  156.6 0.6 fusion.53
  157.2 0.0 collective-permute-done
  157.2 0.0 collective-permute-done.1
  157.2 1.1 pad_maximum_fusion
  158.3 3.5 %collective-permute-start.2 = (bf16[2,2,256,256]{3,2,1,0:T(8,128)(2,1)S(1)}, bf16[2,2,256,256]{3,2,1,0:T(8,128)(2,1)S(1)}, u32[]{:S(2)}, u32[]{:S(2)}) collective-permute-start(bf16[2,2,256,256]{3,2,1,0:T(8,128)(2,1)S(1)} %pad_maximum_fusion), channel_id=1, source_target_pairs={{0,4},{4,8},{8,12},{1,5},{5,9},{9,13},{2,6},{6,10},{10,14},{3,7},{... | collective-permute-start | bytes 1572872 | tf_op jit(solution)/shard_map/ppermute | solution.py:22
  161.8 1.3 collective-permute-start.3
  163.1 0.0 collective-permute-done.4
  163.1 0.0 collective-permute-done.5
  163.1 2.5 %multiply_convert_fusion.1 = (bf16[2,256,256]{2,1,0:T(8,128)(2,1)S(1)}, bf16[2,256,256]{2,1,0:T(8,128)(2,1)S(1)}) fusion(f32[]{:T(128)} %bitcast.22, bf16[2,256,256]{2,1,0:T(8,128)(2,1)S(1)} %collective-permute-done.5, f32[6,256,256]{2,1,0:T(8,128)} %get-tuple-element.11, bf16[2,256,256]{2,1,0:T(8,128)(2,1)S(1)} %collective-permute-done.4, f32[]{:T(128)} %bitcast.23), kind=kLoop, calls=%fused_computation.31 | loop fusion | flops 1048576 | bytes 1572872 | tf_op jit(solution)/shard_map/convert_element_type | solution.py:107
  165.6 5.3 %collective-permute-start.6 = (bf16[2,256,256]{2,1,0:T(8,128)(2,1)S(1)}, bf16[2,256,256]{2,1,0:T(8,128)(2,1)S(1)}, u32[]{:S(2)}, u32[]{:S(2)}) collective-permute-start(bf16[2,256,256]{2,1,0:T(8,128)(2,1)S(1)} %get-tuple-element.14), channel_id=1, source_target_pairs={{0,2},{1,3},{4,6},{5,7},{8,10},{9,11},{12,14},{13,15},{16,18},{17,... | collective-permute-start | bytes 786440 | tf_op jit(solution)/shard_map/ppermute | solution.py:22
  170.9 1.5 collective-permute-start.7
  172.4 2.9 %collective-permute-done.6 = bf16[2,256,256]{2,1,0:T(8,128)(2,1)S(1)} collective-permute-done((bf16[2,256,256]{2,1,0:T(8,128)(2,1)S(1)}, bf16[2,256,256]{2,1,0:T(8,128)(2,1)S(1)}, u32[]{:S(2)}, u32[]{:S(2)}) %collective-permute-start.6) | collective-permute-done | bytes 262176 | tf_op jit(solution)/shard_map/ppermute | solution.py:22
  175.3 4.1 %collective-permute-done.7 = bf16[2,256,256]{2,1,0:T(8,128)(2,1)S(1)} collective-permute-done((bf16[2,256,256]{2,1,0:T(8,128)(2,1)S(1)}, bf16[2,256,256]{2,1,0:T(8,128)(2,1)S(1)}, u32[]{:S(2)}, u32[]{:S(2)}) %collective-permute-start.7) | collective-permute-done | bytes 262176 | tf_op jit(solution)/shard_map/ppermute | solution.py:22
  179.4 0.1 convert_add_fusion
  179.5 0.0 collective-permute-done.2
  179.5 0.0 collective-permute-done.3
  179.5 1.8 multiply_bitcast_fusion
  181.3 4.7 %gather_fusion = bf16[18,2,340,256]{3,2,1,0:T(8,128)(2,1)} fusion(bf16[2,6,340,256]{3,2,1,0:T(8,128)(2,1)S(1)} %multiply_bitcast_fusion, s32[1024]{0:T(1024)S(1)} %pad_clamp_fusion), kind=kCustom, calls=%fused_computation | custom fusion | bytes 12533832 | tf_op jit(solution)/shard_map/gather | solution.py:78
  186.0 5.9 %fusion.21 = f32[2,256,128]{2,1,0:T(8,128)S(1)} fusion(bf16[2,128,9,340]{1,0,3,2:T(2,128)(2,1)} %bitcast.78, bf16[2,9,2,340,256]{4,3,2,1,0:T(8,128)(2,1)} %bitcast.74, bf16[2,128]{1,0:T(2,128)(2,1)S(1)} %fusion.48), kind=kOutput, calls=%fused_computation.23 | convolution fusion | flops 803009536 | bytes 8096256 | tf_op jit(solution)/shard_map/apkm,jakmc->japc/dot_general | solution.py:88
  191.9 0.0 copy-start.1
  191.9 0.1 copy.36
  192.1 0.1 fusion.30
  192.1 0.0 copy-start
  192.2 0.8 copy-done
  193.0 0.0 reduce-scatter.2.cloned.1.call-update
  193.0 4.6 %fusion.14 = bf16[9,340,2,128]{3,1,0,2:T(8,128)(2,1)S(1)} fusion(f32[2,128]{1,0:T(2,128)S(1)} %convert_multiply_fusion, bf16[2,2,9,340,256]{4,3,0,2,1:T(8,128)(2,1)} %bitcast.75, bf16[2,128,256]{2,1,0:T(8,128)(2,1)S(1)} %dynamic-slice_bitcast_fusion), kind=kOutput, calls=%fused_computation.20 | convolution fusion | flops 803727360 | bytes 7965696 | tf_op jit(solution)/shard_map/jakmc,japc->kmap/dot_general | solution.py:80
  197.7 0.3 convert_element_type.74
  198.0 12.1 %copy.37 = bf16[1,2,128,3060]{2,1,3,0:T(2,128)(2,1)} copy(bf16[1,2,128,3060]{2,3,1,0:T(8,128)(2,1)S(1)} %bitcast.76) | data formatting | bytes 3133440
  (22 shorter events, 0.3 us)
Async XLA Ops:
  7.2 202.9 %reduce-scatter.2.cloned.1.call-start = ((), (), s32[]{:S(2)}) async-start(), calls=%async_computation.1 | async-start | bytes 786432 | tf_op jit(solution)/shard_map/reduce_scatter | solution.py:112
  9.6 147.7 %collective-permute-start = (bf16[2,256,256]{2,1,0:T(8,128)(2,1)S(1)}, bf16[2,256,256]{2,1,0:T(8,128)(2,1)}, u32[]{:S(2)}, u32[]{:S(2)}) collective-permute-start(bf16[2,256,256]{2,1,0:T(8,128)(2,1)S(1)} %bitcast.79), channel_id=1, source_target_pairs={{0,2},{1,3},{4,6},{5,7},{8,10},{9,11},{12,14},{13,15},{16,18},{17,... | collective-permute-start | bytes 786440 | tf_op jit(solution)/shard_map/ppermute | solution.py:22
  15.0 142.2 %collective-permute-start.1 = (bf16[2,256,256]{2,1,0:T(8,128)(2,1)S(1)}, bf16[2,256,256]{2,1,0:T(8,128)(2,1)}, u32[]{:S(2)}, u32[]{:S(2)}) collective-permute-start(bf16[2,256,256]{2,1,0:T(8,128)(2,1)S(1)} %bitcast.80), channel_id=1, source_target_pairs={{2,0},{3,1},{6,4},{7,5},{10,8},{11,9},{14,12},{15,13},{18,16},{19,... | collective-permute-start | bytes 786440 | tf_op jit(solution)/shard_map/ppermute | solution.py:22
  19.4 5.9 %copy-start.2 = (s32[2,9]{1,0:T(2,128)S(1)}, s32[2,9]{1,0:T(2,128)}, u32[]{:S(2)}) copy-start(s32[2,9]{1,0:T(2,128)} %param.6) | copy-start | bytes 220
  147.2 9.3 %copy-start.3 = (s32[1,2]{1,0:T(1,128)S(1)}, s32[1,2]{1,0:T(1,128)}, u32[]{:S(2)}) copy-start(s32[1,2]{1,0:T(1,128)} %param.7) | copy-start | bytes 28
  150.6 12.5 %collective-permute-start.4 = (bf16[2,256,256]{2,1,0:T(8,128)(2,1)S(1)}, bf16[2,256,256]{2,1,0:T(8,128)(2,1)S(1)}, u32[]{:S(2)}, u32[]{:S(2)}) collective-permute-start(bf16[2,256,256]{2,1,0:T(8,128)(2,1)S(1)} %get-tuple-element.16), channel_id=1, source_target_pairs={{4,0},{8,4},{12,8},{5,1},{9,5},{13,9},{6,2},{10,6},{14,10},{7,3},{... | collective-permute-start | bytes 786440 | tf_op jit(solution)/shard_map/ppermute | solution.py:22
  151.9 11.3 %collective-permute-start.5 = (bf16[2,256,256]{2,1,0:T(8,128)(2,1)S(1)}, bf16[2,256,256]{2,1,0:T(8,128)(2,1)S(1)}, u32[]{:S(2)}, u32[]{:S(2)}) collective-permute-start(bf16[2,256,256]{2,1,0:T(8,128)(2,1)S(1)} %get-tuple-element.17), channel_id=1, source_target_pairs={{0,4},{4,8},{8,12},{1,5},{5,9},{9,13},{2,6},{6,10},{10,14},{3,7},{... | collective-permute-start | bytes 786440 | tf_op jit(solution)/shard_map/ppermute | solution.py:22
  158.3 21.2 %collective-permute-start.2 = (bf16[2,2,256,256]{3,2,1,0:T(8,128)(2,1)S(1)}, bf16[2,2,256,256]{3,2,1,0:T(8,128)(2,1)S(1)}, u32[]{:S(2)}, u32[]{:S(2)}) collective-permute-start(bf16[2,2,256,256]{3,2,1,0:T(8,128)(2,1)S(1)} %pad_maximum_fusion), channel_id=1, source_target_pairs={{0,4},{4,8},{8,12},{1,5},{5,9},{9,13},{2,6},{6,10},{10,14},{3,7},{... | collective-permute-start | bytes 1572872 | tf_op jit(solution)/shard_map/ppermute | solution.py:22
  161.8 17.7 %collective-permute-start.3 = (bf16[2,2,256,256]{3,2,1,0:T(8,128)(2,1)S(1)}, bf16[2,2,256,256]{3,2,1,0:T(8,128)(2,1)S(1)}, u32[]{:S(2)}, u32[]{:S(2)}) collective-permute-start(bf16[2,2,256,256]{3,2,1,0:T(8,128)(2,1)S(1)} %pad_maximum_fusion), channel_id=1, source_target_pairs={{4,0},{8,4},{12,8},{5,1},{9,5},{13,9},{6,2},{10,6},{14,10},{7,3},{... | collective-permute-start | bytes 1572872 | tf_op jit(solution)/shard_map/ppermute | solution.py:22
  165.6 9.7 %collective-permute-start.6 = (bf16[2,256,256]{2,1,0:T(8,128)(2,1)S(1)}, bf16[2,256,256]{2,1,0:T(8,128)(2,1)S(1)}, u32[]{:S(2)}, u32[]{:S(2)}) collective-permute-start(bf16[2,256,256]{2,1,0:T(8,128)(2,1)S(1)} %get-tuple-element.14), channel_id=1, source_target_pairs={{0,2},{1,3},{4,6},{5,7},{8,10},{9,11},{12,14},{13,15},{16,18},{17,... | collective-permute-start | bytes 786440 | tf_op jit(solution)/shard_map/ppermute | solution.py:22
  170.9 8.6 %collective-permute-start.7 = (bf16[2,256,256]{2,1,0:T(8,128)(2,1)S(1)}, bf16[2,256,256]{2,1,0:T(8,128)(2,1)S(1)}, u32[]{:S(2)}, u32[]{:S(2)}) collective-permute-start(bf16[2,256,256]{2,1,0:T(8,128)(2,1)S(1)} %get-tuple-element.15), channel_id=1, source_target_pairs={{2,0},{3,1},{6,4},{7,5},{10,8},{11,9},{14,12},{15,13},{18,16},{19,... | collective-permute-start | bytes 786440 | tf_op jit(solution)/shard_map/ppermute | solution.py:22
  191.9 1.0 copy-start.1
  192.1 0.8 copy-start
Sparse Core Ops, SparseCore 0:
  193.1 8.8 reduce-scatter.1

commit v2 on v1

--- a/solution.py
+++ b/solution.py
@@ -93,7 +93,11 @@
     member = (
         slot_ids[:, :, None] == jnp.arange(3 * tile_count, dtype=jnp.int32)[None, None, :]
     ).astype(jnp.float32)
-    cells = jnp.sum(member[:, :, :, None, None] * base_grad[:, :, None], axis=(0, 1))
+    cells = None
+    for a in range(tile_count):
+        for k in range(NEIGHBOURS):
+            term = member[a, k][:, None, None] * base_grad[a, k][None]
+            cells = term if cells is None else cells + term
     window_grad = pool_back(cells)
     sent_left = shift(window_grad[:tile_count].astype(jnp.bfloat16), "tile", -1)
     sent_right = shift(window_grad[2 * tile_count :].astype(jnp.bfloat16), "tile", 1)

time: 218 us -> 109 us (0.50)
  other arithmetic: 120 us -> 13.2 us
  local copies, waits for them, and re-layouts: 34.2 us -> 31.3 us
    reduce_sum x1 -> x0, other arithmetic: 112 us -> none  [local(): jnp.sum(member[:, :, :, None, None] * base_grad[:, :, None], axis=(0, 1))]
    dot_general x1 -> x0, local copies, waits for them, and re-layouts: 5.87 us -> none  [local(): jnp.einsum('apkm,apc->akmc', upstream, queries, preferred_element_type=jn...]
    add x0 -> x1, other arithmetic: none -> 5.22 us  [local(): cells = term if cells is None else cells + term]
    mul x0 -> x2, local copies, waits for them, and re-layouts: none -> 2.28 us  [local(): term = member[a, k][:, None, None] * base_grad[a, k][None]]
  transfers between devices with their start and end apart: 9 -> 9, of which waited for: 2 -> 2; matrix products, arithmetic and copies ran while one was open for 72% -> 42% of each run, Pallas kernels for 0% -> 0%
where the time goes in v2:
time: 109 us
  local copies, waits for them, and re-layouts  31.3 us (29%)
  starting transfers between devices  23.9 us (22%)
  matrix products  14.7 us (13%)
  between operations  14.3 us (13%)
  other arithmetic  13.2 us (12%)
  waiting for transfers between devices  7.29 us (7%)
  blocking collectives  3.91 us (4%)
    ppermute x8, starting transfers between devices, shift(): return lax.ppermute(x, axis, pairs)  23.9 us
    unnamed x9, local copies, waits for them, and re-layouts  12.9 us
    ppermute x8, waiting for transfers between devices, shift(): return lax.ppermute(x, axis, pairs)  7.27 us
    reshape x2, local copies, waits for them, and re-layouts, pool_back(): part = part.reshape(lead, PIXELS, chans)  5.93 us
    dot_general x1, matrix products, local(): jnp.einsum('apkm,jakmc->japc', upstream, chosen, preferred_element_type=j...  5.91 us
    add x1, other arithmetic, local(): cells = term if cells is None else cells + term  5.22 us
    gather x1, local copies, waits for them, and re-layouts, local(): chosen = pyramid[:, slot_ids]  4.65 us
    dot_general x1, matrix products, local(): jnp.einsum('jakmc,japc->kmap', chosen, queries2, preferred_element_type=j...  4.64 us
  transfers between devices with their start and end apart: 9, of which 2 were waited for; matrix products, arithmetic and copies ran while one was open for 42% of the time, Pallas kernels for 0%

profile of v2, /device:TPU:0, one launch (start us, length us, event | category | flops | bytes accessed | tf_op | source)
XLA Modules:
  0.0 108.7 jit_solution(3062728281193975906)
XLA Ops:
  7.2 0.0 reduce-scatter.2.cloned.1.call-start
  7.2 3.9 %all_gather.3 = bf16[1,2,256,256]{3,2,1,0:T(8,128)(2,1)} all-gather(bf16[1,2,256,128]{3,2,1,0:T(8,128)(2,1)} %param.5), channel_id=1, replica_groups=mesh['clip'=2,'tile'=4,'frame'=2,'chan'=2] {'chan'}, dimensions={3}, use_global_device_ids=true | all-gather | bytes 393216 | tf_op jit(solution)/shard_map/all_gather | solution.py:58
  11.1 5.2 %collective-permute-start = (bf16[2,256,256]{2,1,0:T(8,128)(2,1)}, bf16[2,256,256]{2,1,0:T(8,128)(2,1)}, u32[]{:S(2)}, u32[]{:S(2)}) collective-permute-start(bf16[2,256,256]{2,1,0:T(8,128)(2,1)} %bitcast.2), channel_id=1, source_target_pairs={{0,2},{1,3},{4,6},{5,7},{8,10},{9,11},{12,14},{13,15},{16,18},{17,... | collective-permute-start | bytes 786440 | tf_op jit(solution)/shard_map/ppermute | solution.py:22
  16.4 1.3 %collective-permute-start.1 = (bf16[2,256,256]{2,1,0:T(8,128)(2,1)}, bf16[2,256,256]{2,1,0:T(8,128)(2,1)}, u32[]{:S(2)}, u32[]{:S(2)}) collective-permute-start(bf16[2,256,256]{2,1,0:T(8,128)(2,1)} %bitcast.2), channel_id=1, source_target_pairs={{2,0},{3,1},{6,4},{7,5},{10,8},{11,9},{14,12},{15,13},{18,16},{19,... | collective-permute-start | bytes 786440 | tf_op jit(solution)/shard_map/ppermute | solution.py:22
  17.6 0.7 fusion.48
  18.3 2.4 %fusion.20 = f32[2,9,340,256]{3,2,1,0:T(8,128)S(1)} fusion(bf16[2,128,9,340]{1,0,3,2:T(2,128)(2,1)} %bitcast.149, bf16[2,128]{1,0:T(2,128)(2,1)S(1)} %fusion.48, bf16[1,2,256,256]{3,2,1,0:T(8,128)(2,1)} %all_gather.3, s32[]{:T(128)S(6)} %select_n.104), kind=kOutput, calls=%fused_computation.22 | convolution fusion | flops 401863680 | bytes 7965188 | tf_op jit(solution)/shard_map/apkm,apc->akmc/dot_general | solution.py:92
  20.7 0.0 copy-start.2
  20.7 2.3 %slice_bitcast_fusion.17 = (f32[340,256]{1,0:T(8,128)S(1)}, f32[340,256]{1,0:T(8,128)S(1)}, f32[340,256]{1,0:T(8,128)S(1)}, f32[340,256]{1,0:T(8,128)S(1)}, f32[...) fusion(f32[2,9,340,256]{3,2,1,0:T(8,128)S(1)} %fusion.20), kind=kLoop, calls=%fused_computation.51 | loop fusion | bytes 12533760 | tf_op jit(solution)/shard_map/mul | solution.py:99
  23.0 0.0 copy-done.2
  23.0 0.1 fusion.41
  23.1 5.2 %multiply_add_fusion = f32[6,340,256]{2,1,0:T(8,128)S(1)} fusion(f32[340,256]{1,0:T(8,128)S(1)} %get-tuple-element.15, f32[6]{0:T(128)S(1)} %get-tuple-element.37, f32[340,256]{1,0:T(8,128)S(1)} %get-tuple-element.16, f32[6]{0:T(128)S(1)} %get-tuple-element.38, f32[340,256]{1,0:T(8,128)S(1)} %get-tuple-element.17, f32[6]{0:T(128)S(1)} %get-tuple-element.39, ...), kind=kLoop, calls=%fused_computation.6 | loop fusion | flops 18278400 | bytes 8356272 | tf_op jit(solution)/shard_map/add | solution.py:100
  28.4 1.9 %broadcast_in_dim.27 = f32[6,8,2,8,2,256]{5,4,3,2,1,0:T(2,128)} broadcast(f32[6,8,8,256]{3,2,1,0:T(8,128)S(1)} %fusion.29), dimensions={0,1,3,5} | broadcast | bytes 1966080 | tf_op jit(solution)/shard_map/broadcast_in_dim | solution.py:48
  30.3 3.2 %reshape.179 = f32[6,256,256]{2,1,0:T(8,128)} reshape(f32[6,8,2,8,2,256]{5,4,3,2,1,0:T(2,128)} %broadcast_in_dim.27) | data formatting | bytes 3145728 | tf_op jit(solution)/shard_map/reshape | solution.py:49
  33.5 1.5 %broadcast_in_dim.29 = f32[6,4,4,4,4,256]{5,4,3,2,1,0:T(4,128)} broadcast(f32[6,4,4,256]{3,2,1,0:T(4,128)S(1)} %broadcast_in_dim.28), dimensions={0,1,3,5} | broadcast | bytes 1671168 | tf_op jit(solution)/shard_map/broadcast_in_dim | solution.py:48
  35.0 2.8 %reshape.180 = f32[6,256,256]{2,1,0:T(8,128)} reshape(f32[6,4,4,4,4,256]{5,4,3,2,1,0:T(4,128)} %broadcast_in_dim.29) | data formatting | bytes 3145728 | tf_op jit(solution)/shard_map/reshape | solution.py:49
  37.8 0.0 copy-start.3
  37.8 3.4 %fusion.50 = (bf16[6,256,256]{2,1,0:T(8,128)(2,1)S(1)}, f32[6,256,256]{2,1,0:T(8,128)}) fusion(f32[6,2,2,256]{3,2,1,0:T(2,128)S(1)} %broadcast_in_dim.60, f32[6,256,256]{2,1,0:T(8,128)} %reshape.180, f32[6,256,256]{2,1,0:T(8,128)} %reshape.179, f32[6,340,256]{2,1,0:T(8,128)S(1)} %multiply_add_fusion), kind=kLoop, calls=%fused_computation.141 | loop fusion | flops 1572864 | bytes 7102464 | tf_op jit(solution)/shard_map/convert.1
  41.3 1.3 %collective-permute-start.4 = (bf16[2,256,256]{2,1,0:T(8,128)(2,1)S(1)}, bf16[2,256,256]{2,1,0:T(8,128)(2,1)S(1)}, u32[]{:S(2)}, u32[]{:S(2)}) collective-permute-start(bf16[2,256,256]{2,1,0:T(8,128)(2,1)S(1)} %get-tuple-element.34), channel_id=1, source_target_pairs={{4,0},{8,4},{12,8},{5,1},{9,5},{13,9},{6,2},{10,6},{14,10},{7,3},{... | collective-permute-start | bytes 786440 | tf_op jit(solution)/shard_map/ppermute | solution.py:22
  42.6 4.6 %collective-permute-start.5 = (bf16[2,256,256]{2,1,0:T(8,128)(2,1)S(1)}, bf16[2,256,256]{2,1,0:T(8,128)(2,1)S(1)}, u32[]{:S(2)}, u32[]{:S(2)}) collective-permute-start(bf16[2,256,256]{2,1,0:T(8,128)(2,1)S(1)} %get-tuple-element.35), channel_id=1, source_target_pairs={{0,4},{4,8},{8,12},{1,5},{5,9},{9,13},{2,6},{6,10},{10,14},{3,7},{... | collective-permute-start | bytes 786440 | tf_op jit(solution)/shard_map/ppermute | solution.py:22
  47.2 0.0 copy-done.3
  47.2 0.1 reshape.184
  47.3 0.6 fusion.53
  47.9 0.0 collective-permute-done
  47.9 0.0 collective-permute-done.1
  47.9 1.1 pad_maximum_fusion
  49.0 3.5 %collective-permute-start.2 = (bf16[2,2,256,256]{3,2,1,0:T(8,128)(2,1)S(1)}, bf16[2,2,256,256]{3,2,1,0:T(8,128)(2,1)S(1)}, u32[]{:S(2)}, u32[]{:S(2)}) collective-permute-start(bf16[2,2,256,256]{3,2,1,0:T(8,128)(2,1)S(1)} %pad_maximum_fusion), channel_id=1, source_target_pairs={{0,4},{4,8},{8,12},{1,5},{5,9},{9,13},{2,6},{6,10},{10,14},{3,7},{... | collective-permute-start | bytes 1572872 | tf_op jit(solution)/shard_map/ppermute | solution.py:22
  52.5 1.3 %collective-permute-start.3 = (bf16[2,2,256,256]{3,2,1,0:T(8,128)(2,1)S(1)}, bf16[2,2,256,256]{3,2,1,0:T(8,128)(2,1)S(1)}, u32[]{:S(2)}, u32[]{:S(2)}) collective-permute-start(bf16[2,2,256,256]{3,2,1,0:T(8,128)(2,1)S(1)} %pad_maximum_fusion), channel_id=1, source_target_pairs={{4,0},{8,4},{12,8},{5,1},{9,5},{13,9},{6,2},{10,6},{14,10},{7,3},{... | collective-permute-start | bytes 1572872 | tf_op jit(solution)/shard_map/ppermute | solution.py:22
  53.8 0.0 collective-permute-done.4
  53.8 0.0 collective-permute-done.5
  53.8 2.5 %multiply_convert_fusion.1 = (bf16[2,256,256]{2,1,0:T(8,128)(2,1)S(1)}, bf16[2,256,256]{2,1,0:T(8,128)(2,1)S(1)}) fusion(f32[]{:T(128)} %bitcast.58, bf16[2,256,256]{2,1,0:T(8,128)(2,1)S(1)} %collective-permute-done.5, f32[6,256,256]{2,1,0:T(8,128)} %get-tuple-element.11, bf16[2,256,256]{2,1,0:T(8,128)(2,1)S(1)} %collective-permute-done.4, f32[]{:T(128)} %bitcast.59), kind=kLoop, calls=%fused_computation.31 | loop fusion | flops 1048576 | bytes 1572872 | tf_op jit(solution)/shard_map/convert_element_type | solution.py:111
  56.3 5.3 %collective-permute-start.6 = (bf16[2,256,256]{2,1,0:T(8,128)(2,1)S(1)}, bf16[2,256,256]{2,1,0:T(8,128)(2,1)S(1)}, u32[]{:S(2)}, u32[]{:S(2)}) collective-permute-start(bf16[2,256,256]{2,1,0:T(8,128)(2,1)S(1)} %get-tuple-element.32), channel_id=1, source_target_pairs={{0,2},{1,3},{4,6},{5,7},{8,10},{9,11},{12,14},{13,15},{16,18},{17,... | collective-permute-start | bytes 786440 | tf_op jit(solution)/shard_map/ppermute | solution.py:22
  61.6 1.5 %collective-permute-start.7 = (bf16[2,256,256]{2,1,0:T(8,128)(2,1)S(1)}, bf16[2,256,256]{2,1,0:T(8,128)(2,1)S(1)}, u32[]{:S(2)}, u32[]{:S(2)}) collective-permute-start(bf16[2,256,256]{2,1,0:T(8,128)(2,1)S(1)} %get-tuple-element.33), channel_id=1, source_target_pairs={{2,0},{3,1},{6,4},{7,5},{10,8},{11,9},{14,12},{15,13},{18,16},{19,... | collective-permute-start | bytes 786440 | tf_op jit(solution)/shard_map/ppermute | solution.py:22
  63.1 3.1 %collective-permute-done.6 = bf16[2,256,256]{2,1,0:T(8,128)(2,1)S(1)} collective-permute-done((bf16[2,256,256]{2,1,0:T(8,128)(2,1)S(1)}, bf16[2,256,256]{2,1,0:T(8,128)(2,1)S(1)}, u32[]{:S(2)}, u32[]{:S(2)}) %collective-permute-start.6) | collective-permute-done | bytes 262176 | tf_op jit(solution)/shard_map/ppermute | solution.py:22
  66.2 4.1 %collective-permute-done.7 = bf16[2,256,256]{2,1,0:T(8,128)(2,1)S(1)} collective-permute-done((bf16[2,256,256]{2,1,0:T(8,128)(2,1)S(1)}, bf16[2,256,256]{2,1,0:T(8,128)(2,1)S(1)}, u32[]{:S(2)}, u32[]{:S(2)}) %collective-permute-start.7) | collective-permute-done | bytes 262176 | tf_op jit(solution)/shard_map/ppermute | solution.py:22
  70.3 0.1 convert_add_fusion
  70.4 0.0 collective-permute-done.2
  70.4 0.0 collective-permute-done.3
  70.4 1.8 %multiply_bitcast_fusion = bf16[2,6,340,256]{3,2,1,0:T(8,128)(2,1)S(1)} fusion(bf16[2,2,256,256]{3,2,1,0:T(8,128)(2,1)S(1)} %collective-permute-done.3, bf16[1,2,256,256]{3,2,1,0:T(8,128)(2,1)} %bitcast.4, bf16[1,2,256,256]{3,2,1,0:T(8,128)(2,1)} %bitcast.3, bf16[2,2,256,256]{3,2,1,0:T(8,128)(2,1)S(1)} %collective-permute-done.2, ...), kind=kOutput, calls=%fused_computation.7 | convolution fusion | flops 539918336 | bytes 3835908 | tf_op jit(solution)/shard_map/mp,jwpc->jwmc/dot_general | solution.py:65
  72.2 4.6 %gather_fusion = bf16[18,2,340,256]{3,2,1,0:T(8,128)(2,1)} fusion(bf16[2,6,340,256]{3,2,1,0:T(8,128)(2,1)S(1)} %multiply_bitcast_fusion, s32[1024]{0:T(1024)S(1)} %pad_clamp_fusion), kind=kCustom, calls=%fused_computation | custom fusion | bytes 12533832 | tf_op jit(solution)/shard_map/gather | solution.py:78
  76.9 5.9 %fusion.21 = f32[2,256,128]{2,1,0:T(8,128)S(1)} fusion(bf16[2,128,9,340]{1,0,3,2:T(2,128)(2,1)} %bitcast.150, bf16[2,9,2,340,256]{4,3,2,1,0:T(8,128)(2,1)} %bitcast.146, bf16[2,128]{1,0:T(2,128)(2,1)S(1)} %fusion.48), kind=kOutput, calls=%fused_computation.23 | convolution fusion | flops 803009536 | bytes 8096256 | tf_op jit(solution)/shard_map/apkm,jakmc->japc/dot_general | solution.py:88
  82.8 0.1 copy.70
  82.9 0.1 fusion.30
  83.0 0.8 copy-done
  83.8 0.0 reduce-scatter.2.cloned.1.call-update
  83.9 0.9 dynamic-slice_bitcast_fusion
  84.8 4.6 %fusion.14 = bf16[9,340,2,128]{3,1,0,2:T(8,128)(2,1)S(1)} fusion(f32[2,128]{1,0:T(2,128)S(1)} %convert_multiply_fusion, bf16[2,2,9,340,256]{4,3,0,2,1:T(8,128)(2,1)} %bitcast.147, bf16[2,128,256]{2,1,0:T(8,128)(2,1)S(1)} %dynamic-slice_bitcast_fusion), kind=kOutput, calls=%fused_computation.20 | convolution fusion | flops 803727360 | bytes 7965696 | tf_op jit(solution)/shard_map/jakmc,japc->kmap/dot_general | solution.py:80
  89.4 0.3 convert_element_type.70
  89.7 12.1 %copy.71 = bf16[1,2,128,3060]{2,1,3,0:T(2,128)(2,1)} copy(bf16[1,2,128,3060]{2,3,1,0:T(8,128)(2,1)S(1)} %bitcast.148) | data formatting | bytes 3133440
  (22 shorter events, 0.3 us)
Async XLA Ops:
  7.2 94.7 %reduce-scatter.2.cloned.1.call-start = ((), (), s32[]{:S(2)}) async-start(), calls=%async_computation.1 | async-start | bytes 786432 | tf_op jit(solution)/shard_map/reduce_scatter | solution.py:116
  11.1 36.8 %collective-permute-start = (bf16[2,256,256]{2,1,0:T(8,128)(2,1)}, bf16[2,256,256]{2,1,0:T(8,128)(2,1)}, u32[]{:S(2)}, u32[]{:S(2)}) collective-permute-start(bf16[2,256,256]{2,1,0:T(8,128)(2,1)} %bitcast.2), channel_id=1, source_target_pairs={{0,2},{1,3},{4,6},{5,7},{8,10},{9,11},{12,14},{13,15},{16,18},{17,... | collective-permute-start | bytes 786440 | tf_op jit(solution)/shard_map/ppermute | solution.py:22
  16.4 31.6 %collective-permute-start.1 = (bf16[2,256,256]{2,1,0:T(8,128)(2,1)}, bf16[2,256,256]{2,1,0:T(8,128)(2,1)}, u32[]{:S(2)}, u32[]{:S(2)}) collective-permute-start(bf16[2,256,256]{2,1,0:T(8,128)(2,1)} %bitcast.2), channel_id=1, source_target_pairs={{2,0},{3,1},{6,4},{7,5},{10,8},{11,9},{14,12},{15,13},{18,16},{19,... | collective-permute-start | bytes 786440 | tf_op jit(solution)/shard_map/ppermute | solution.py:22
  20.7 2.3 %copy-start.2 = (s32[2,9]{1,0:T(2,128)S(1)}, s32[2,9]{1,0:T(2,128)}, u32[]{:S(2)}) copy-start(s32[2,9]{1,0:T(2,128)} %param.6) | copy-start | bytes 220
  37.8 9.3 %copy-start.3 = (s32[1,2]{1,0:T(1,128)S(1)}, s32[1,2]{1,0:T(1,128)}, u32[]{:S(2)}) copy-start(s32[1,2]{1,0:T(1,128)} %param.7) | copy-start | bytes 28
  41.3 12.6 %collective-permute-start.4 = (bf16[2,256,256]{2,1,0:T(8,128)(2,1)S(1)}, bf16[2,256,256]{2,1,0:T(8,128)(2,1)S(1)}, u32[]{:S(2)}, u32[]{:S(2)}) collective-permute-start(bf16[2,256,256]{2,1,0:T(8,128)(2,1)S(1)} %get-tuple-element.34), channel_id=1, source_target_pairs={{4,0},{8,4},{12,8},{5,1},{9,5},{13,9},{6,2},{10,6},{14,10},{7,3},{... | collective-permute-start | bytes 786440 | tf_op jit(solution)/shard_map/ppermute | solution.py:22
  42.6 11.3 %collective-permute-start.5 = (bf16[2,256,256]{2,1,0:T(8,128)(2,1)S(1)}, bf16[2,256,256]{2,1,0:T(8,128)(2,1)S(1)}, u32[]{:S(2)}, u32[]{:S(2)}) collective-permute-start(bf16[2,256,256]{2,1,0:T(8,128)(2,1)S(1)} %get-tuple-element.35), channel_id=1, source_target_pairs={{0,4},{4,8},{8,12},{1,5},{5,9},{9,13},{2,6},{6,10},{10,14},{3,7},{... | collective-permute-start | bytes 786440 | tf_op jit(solution)/shard_map/ppermute | solution.py:22
  49.0 21.4 %collective-permute-start.2 = (bf16[2,2,256,256]{3,2,1,0:T(8,128)(2,1)S(1)}, bf16[2,2,256,256]{3,2,1,0:T(8,128)(2,1)S(1)}, u32[]{:S(2)}, u32[]{:S(2)}) collective-permute-start(bf16[2,2,256,256]{3,2,1,0:T(8,128)(2,1)S(1)} %pad_maximum_fusion), channel_id=1, source_target_pairs={{0,4},{4,8},{8,12},{1,5},{5,9},{9,13},{2,6},{6,10},{10,14},{3,7},{... | collective-permute-start | bytes 1572872 | tf_op jit(solution)/shard_map/ppermute | solution.py:22
  52.5 17.9 %collective-permute-start.3 = (bf16[2,2,256,256]{3,2,1,0:T(8,128)(2,1)S(1)}, bf16[2,2,256,256]{3,2,1,0:T(8,128)(2,1)S(1)}, u32[]{:S(2)}, u32[]{:S(2)}) collective-permute-start(bf16[2,2,256,256]{3,2,1,0:T(8,128)(2,1)S(1)} %pad_maximum_fusion), channel_id=1, source_target_pairs={{4,0},{8,4},{12,8},{5,1},{9,5},{13,9},{6,2},{10,6},{14,10},{7,3},{... | collective-permute-start | bytes 1572872 | tf_op jit(solution)/shard_map/ppermute | solution.py:22
  56.3 9.9 %collective-permute-start.6 = (bf16[2,256,256]{2,1,0:T(8,128)(2,1)S(1)}, bf16[2,256,256]{2,1,0:T(8,128)(2,1)S(1)}, u32[]{:S(2)}, u32[]{:S(2)}) collective-permute-start(bf16[2,256,256]{2,1,0:T(8,128)(2,1)S(1)} %get-tuple-element.32), channel_id=1, source_target_pairs={{0,2},{1,3},{4,6},{5,7},{8,10},{9,11},{12,14},{13,15},{16,18},{17,... | collective-permute-start | bytes 786440 | tf_op jit(solution)/shard_map/ppermute | solution.py:22
  61.6 8.8 %collective-permute-start.7 = (bf16[2,256,256]{2,1,0:T(8,128)(2,1)S(1)}, bf16[2,256,256]{2,1,0:T(8,128)(2,1)S(1)}, u32[]{:S(2)}, u32[]{:S(2)}) collective-permute-start(bf16[2,256,256]{2,1,0:T(8,128)(2,1)S(1)} %get-tuple-element.33), channel_id=1, source_target_pairs={{2,0},{3,1},{6,4},{7,5},{10,8},{11,9},{14,12},{15,13},{18,16},{19,... | collective-permute-start | bytes 786440 | tf_op jit(solution)/shard_map/ppermute | solution.py:22
  76.9 6.9 %copy-start.1 = (s32[2,256]{1,0:T(2,128)S(1)}, s32[2,256]{1,0:T(2,128)}, u32[]{:S(2)}) copy-start(s32[2,256]{1,0:T(2,128)} %param.8) | copy-start | bytes 6148
  83.0 0.8 copy-start
Sparse Core Ops, SparseCore 0:
  83.9 8.6 reduce-scatter.1

commit v3 on v2

--- a/solution.py
+++ b/solution.py
@@ -20,6 +20,18 @@
     else:
         pairs = [(i + 1, i) for i in range(count - 1)]
     return lax.ppermute(x, axis, pairs)
+
+
+def shift2(x, frame_step, tile_step):
+    frames = lax.axis_size("frame")
+    tiles = lax.axis_size("tile")
+    pairs = []
+    for f in range(frames):
+        for t in range(tiles):
+            f2, t2 = f + frame_step, t + tile_step
+            if 0 <= f2 < frames and 0 <= t2 < tiles:
+                pairs.append((t * frames + f, t2 * frames + f2))
+    return lax.ppermute(x, ("tile", "frame"), pairs)
 
 
 def pool_weights_table():
@@ -56,12 +68,12 @@
     half_rows = cotangent.shape[2]
     pool_weights = pool_weights_table()
     present = lax.all_gather(features, "chan", axis=3, tiled=True)[0]
-    before = shift(present, "frame", 1)
-    after = shift(present, "frame", -1)
-    partners = jnp.stack([before, after], 0)
-    window = jnp.concatenate(
-        [shift(partners, "tile", 1), partners, shift(partners, "tile", -1)], axis=1
-    )
+    rows = []
+    for frame_step in (1, -1):
+        rows.append(
+            jnp.concatenate([shift2(present, frame_step, t) for t in (1, 0, -1)], axis=0)
+        )
+    window = jnp.stack(rows, 0)
     pyramid = jnp.einsum(
         "mp,jwpc->jwmc",
         pool_weights.astype(jnp.bfloat16),
@@ -99,17 +111,13 @@
             term = member[a, k][:, None, None] * base_grad[a, k][None]
             cells = term if cells is None else cells + term
     window_grad = pool_back(cells)
-    sent_left = shift(window_grad[:tile_count].astype(jnp.bfloat16), "tile", -1)
-    sent_right = shift(window_grad[2 * tile_count :].astype(jnp.bfloat16), "tile", 1)
-    returned = (
-        sent_left.astype(jnp.float32)
-        + window_grad[tile_count : 2 * tile_count]
-        + sent_right.astype(jnp.float32)
-    )
     gates = pairing[0].astype(jnp.float32) * (1.0 / math.sqrt(CHANNELS))
-    from_next = shift((returned * gates[0]).astype(jnp.bfloat16), "frame", -1)
-    from_prev = shift((returned * gates[1]).astype(jnp.bfloat16), "frame", 1)
-    key_grad = from_prev.astype(jnp.float32) + from_next.astype(jnp.float32)
+    key_grad = None
+    for j, frame_step in ((0, -1), (1, 1)):
+        for block, tile_step in ((0, -1), (1, 0), (2, 1)):
+            piece = window_grad[block * tile_count : (block + 1) * tile_count] * gates[j]
+            got = shift2(piece.astype(jnp.bfloat16), frame_step, tile_step).astype(jnp.float32)
+            key_grad = got if key_grad is None else key_grad + got
     placed = lax.dynamic_update_slice_in_dim(
         jnp.zeros(key_grad.shape, jnp.float32), query_grad, core_index * half_rows, 1
     )

time: 109 us -> 117 us (1.073)
  the two profiles are of different devices: /device:TPU:0 before, /device:TPU:14 now
where the time goes in v3:
time: 117 us
  local copies, waits for them, and re-layouts  32.2 us (28%)
  starting transfers between devices  31.4 us (27%)
  other arithmetic  18.1 us (15%)
  matrix products  14.5 us (12%)
  between operations  14.4 us (12%)
  blocking collectives  3.57 us (3%)
  waiting for transfers between devices  2.69 us (2%)
    ppermute x12, starting transfers between devices, shift2(): return lax.ppermute(x, ('tile', 'frame'), pairs)  31.4 us
    unnamed x19, local copies, waits for them, and re-layouts  13.5 us
    dot_general x1, matrix products, local(): jnp.einsum('apkm,jakmc->japc', upstream, chosen, preferred_element_type=j...  5.91 us
    reshape x2, local copies, waits for them, and re-layouts, pool_back(): part = part.reshape(lead, PIXELS, chans)  5.89 us
    add x1, other arithmetic, local(): cells = term if cells is None else cells + term  5.22 us
    gather x1, local copies, waits for them, and re-layouts, local(): chosen = pyramid[:, slot_ids]  4.8 us
    dot_general x1, matrix products, local(): jnp.einsum('jakmc,japc->kmap', chosen, queries2, preferred_element_type=j...  4.64 us
    all_gather x1, blocking collectives, local(): present = lax.all_gather(features, 'chan', axis=3, tiled=True)[0]  3.57 us
  transfers between devices with their start and end apart: 13, of which 1 were waited for; matrix products, arithmetic and copies ran while one was open for 53% of the time, Pallas kernels for 0%

profile of v3, /device:TPU:14, one launch (start us, length us, event | category | flops | bytes accessed | tf_op | source)
XLA Modules:
  0.0 116.7 jit_solution(6755023319025698501)
XLA Ops:
  7.2 0.0 reduce-scatter.2.cloned.1.call-start
  7.2 3.6 %all_gather.3 = bf16[1,2,256,256]{3,2,1,0:T(8,128)(2,1)} all-gather(bf16[1,2,256,128]{3,2,1,0:T(8,128)(2,1)} %param.5), channel_id=1, replica_groups=mesh['clip'=2,'tile'=4,'frame'=2,'chan'=2] {'chan'}, dimensions={3}, use_global_device_ids=true | all-gather | bytes 393216 | tf_op jit(solution)/shard_map/all_gather | solution.py:70
  10.8 1.3 %collective-permute-start = (bf16[2,256,256]{2,1,0:T(8,128)(2,1)}, bf16[2,256,256]{2,1,0:T(8,128)(2,1)}, u32[]{:S(2)}, u32[]{:S(2)}) collective-permute-start(bf16[2,256,256]{2,1,0:T(8,128)(2,1)} %bitcast.2), channel_id=1, source_target_pairs={{0,6},{4,10},{8,14},{1,7},{5,11},{9,15},{16,22},{20,26},{24,30},{1... | collective-permute-start | bytes 786440 | tf_op jit(solution)/shard_map/ppermute | solution.py:34
  12.1 1.3 %collective-permute-start.1 = (bf16[2,256,256]{2,1,0:T(8,128)(2,1)}, bf16[2,256,256]{2,1,0:T(8,128)(2,1)}, u32[]{:S(2)}, u32[]{:S(2)}) collective-permute-start(bf16[2,256,256]{2,1,0:T(8,128)(2,1)} %bitcast.2), channel_id=1, source_target_pairs={{0,2},{4,6},{8,10},{12,14},{1,3},{5,7},{9,11},{13,15},{16,18},{20,... | collective-permute-start | bytes 786440 | tf_op jit(solution)/shard_map/ppermute | solution.py:34
  13.4 1.3 %collective-permute-start.2 = (bf16[2,256,256]{2,1,0:T(8,128)(2,1)}, bf16[2,256,256]{2,1,0:T(8,128)(2,1)}, u32[]{:S(2)}, u32[]{:S(2)}) collective-permute-start(bf16[2,256,256]{2,1,0:T(8,128)(2,1)} %bitcast.2), channel_id=1, source_target_pairs={{4,2},{8,6},{12,10},{5,3},{9,7},{13,11},{20,18},{24,22},{28,26},{2... | collective-permute-start | bytes 786440 | tf_op jit(solution)/shard_map/ppermute | solution.py:34
  14.7 9.4 %collective-permute-start.3 = (bf16[2,256,256]{2,1,0:T(8,128)(2,1)}, bf16[2,256,256]{2,1,0:T(8,128)(2,1)}, u32[]{:S(2)}, u32[]{:S(2)}) collective-permute-start(bf16[2,256,256]{2,1,0:T(8,128)(2,1)} %bitcast.2), channel_id=1, source_target_pairs={{2,4},{6,8},{10,12},{3,5},{7,9},{11,13},{18,20},{22,24},{26,28},{1... | collective-permute-start | bytes 786440 | tf_op jit(solution)/shard_map/ppermute | solution.py:34
  24.0 2.0 %collective-permute-start.4 = (bf16[2,256,256]{2,1,0:T(8,128)(2,1)}, bf16[2,256,256]{2,1,0:T(8,128)(2,1)}, u32[]{:S(2)}, u32[]{:S(2)}) collective-permute-start(bf16[2,256,256]{2,1,0:T(8,128)(2,1)} %bitcast.2), channel_id=1, source_target_pairs={{2,0},{6,4},{10,8},{14,12},{3,1},{7,5},{11,9},{15,13},{18,16},{22,... | collective-permute-start | bytes 786440 | tf_op jit(solution)/shard_map/ppermute | solution.py:34
  26.0 0.7 fusion.43
  26.7 0.6 copy-done.1
  27.3 2.4 %fusion.16 = f32[2,9,340,256]{3,2,1,0:T(8,128)S(1)} fusion(bf16[2,128,9,340]{1,0,3,2:T(2,128)(2,1)} %bitcast.150, bf16[2,128]{1,0:T(2,128)(2,1)S(1)} %fusion.43, bf16[1,2,256,256]{3,2,1,0:T(8,128)(2,1)} %all_gather.3, s32[]{:T(128)S(6)} %select_n.104), kind=kOutput, calls=%fused_computation.18 | convolution fusion | flops 401863680 | bytes 7965188 | tf_op jit(solution)/shard_map/apkm,apc->akmc/dot_general | solution.py:104
  29.7 2.3 %slice_bitcast_fusion.17 = (f32[340,256]{1,0:T(8,128)S(1)}, f32[340,256]{1,0:T(8,128)S(1)}, f32[340,256]{1,0:T(8,128)S(1)}, f32[340,256]{1,0:T(8,128)S(1)}, f32[...) fusion(f32[2,9,340,256]{3,2,1,0:T(8,128)S(1)} %fusion.16), kind=kLoop, calls=%fused_computation.50 | loop fusion | bytes 12533760 | tf_op jit(solution)/shard_map/mul | solution.py:111
  32.0 0.6 compare_select_fusion
  32.6 0.1 fusion.36
  32.6 5.2 %multiply_add_fusion = f32[6,340,256]{2,1,0:T(8,128)S(1)} fusion(f32[340,256]{1,0:T(8,128)S(1)} %get-tuple-element.13, f32[6]{0:T(128)S(1)} %get-tuple-element.37, f32[340,256]{1,0:T(8,128)S(1)} %get-tuple-element.14, f32[6]{0:T(128)S(1)} %get-tuple-element.38, f32[340,256]{1,0:T(8,128)S(1)} %get-tuple-element.15, f32[6]{0:T(128)S(1)} %get-tuple-element.39, ...), kind=kLoop, calls=%fused_computation.6 | loop fusion | flops 18278400 | bytes 8356272 | tf_op jit(solution)/shard_map/add | solution.py:112
  38.0 1.9 %broadcast_in_dim.27 = f32[6,8,2,8,2,256]{5,4,3,2,1,0:T(2,128)} broadcast(f32[6,8,8,256]{3,2,1,0:T(8,128)S(1)} %fusion.24), dimensions={0,1,3,5} | broadcast | bytes 1966080 | tf_op jit(solution)/shard_map/broadcast_in_dim | solution.py:60
  39.9 3.1 %reshape.179 = f32[6,256,256]{2,1,0:T(8,128)} reshape(f32[6,8,2,8,2,256]{5,4,3,2,1,0:T(2,128)} %broadcast_in_dim.27) | data formatting | bytes 3145728 | tf_op jit(solution)/shard_map/reshape | solution.py:61
  43.1 1.6 %broadcast_in_dim.29 = f32[6,4,4,4,4,256]{5,4,3,2,1,0:T(4,128)} broadcast(f32[6,4,4,256]{3,2,1,0:T(4,128)S(1)} %broadcast_in_dim.28), dimensions={0,1,3,5} | broadcast | bytes 1671168 | tf_op jit(solution)/shard_map/broadcast_in_dim | solution.py:60
  44.6 2.7 %reshape.180 = f32[6,256,256]{2,1,0:T(8,128)} reshape(f32[6,4,4,4,4,256]{5,4,3,2,1,0:T(4,128)} %broadcast_in_dim.29) | data formatting | bytes 3145728 | tf_op jit(solution)/shard_map/reshape | solution.py:61
  47.4 0.7 fusion.45
  48.1 0.6 select_convert_fusion
  48.8 0.6 select_convert_fusion.1
  49.4 0.6 select_convert_fusion.2
  49.9 2.2 %fusion.6 = f32[6,256,256]{2,1,0:T(8,128)S(1)} fusion(f32[6,256,256]{2,1,0:T(8,128)} %reshape.180, f32[6,256,256]{2,1,0:T(8,128)} %reshape.179, f32[6,340,256]{2,1,0:T(8,128)S(1)} %multiply_add_fusion, f32[6,2,2,256]{3,2,1,0:T(2,128)S(1)} %broadcast_in_dim.60), kind=kLoop, calls=%fused_computation.12 | loop fusion | flops 1179648 | bytes 6316032 | tf_op jit(solution)/shard_map/add | solution.py:62
  52.2 2.4 %multiply_convert_fusion.5 = (bf16[2,256,256]{2,1,0:T(8,128)(2,1)S(1)}, bf16[2,256,256]{2,1,0:T(8,128)(2,1)S(1)}, bf16[2,256,256]{2,1,0:T(8,128)(2,1)}, bf16[2,2...) fusion(f32[6,256,256]{2,1,0:T(8,128)S(1)} %fusion.6, f32[]{:T(128)} %bitcast.58, ...), kind=kLoop, calls=%fused_computation.30 | loop fusion | flops 1572864 | bytes 3145736 | tf_op jit(solution)/shard_map/convert_element_type | solution.py:119
  54.6 1.3 %collective-permute-start.5 = (bf16[2,256,256]{2,1,0:T(8,128)(2,1)}, bf16[2,256,256]{2,1,0:T(8,128)(2,1)S(1)}, u32[]{:S(2)}, u32[]{:S(2)}) collective-permute-start(bf16[2,256,256]{2,1,0:T(8,128)(2,1)} %bitcast.2), channel_id=1, source_target_pairs={{6,0},{10,4},{14,8},{7,1},{11,5},{15,9},{22,16},{26,20},{30,24},{2... | collective-permute-start | bytes 786440 | tf_op jit(solution)/shard_map/ppermute | solution.py:34
  55.9 0.6 convert_bitcast_fusion
  56.4 0.1 reshape.184
  56.5 0.6 pad_clamp_fusion
  57.1 1.3 %collective-permute-start.10 = (bf16[2,256,256]{2,1,0:T(8,128)(2,1)}, bf16[2,256,256]{2,1,0:T(8,128)(2,1)}, u32[]{:S(2)}, u32[]{:S(2)}) collective-permute-start(bf16[2,256,256]{2,1,0:T(8,128)(2,1)} %get-tuple-element.32), channel_id=1, source_target_pairs={{0,2},{4,6},{8,10},{12,14},{1,3},{5,7},{9,11},{13,15},{16,18},{20,... | collective-permute-start | bytes 786440 | tf_op jit(solution)/shard_map/ppermute | solution.py:34
  58.4 1.3 %collective-permute-start.11 = (bf16[2,256,256]{2,1,0:T(8,128)(2,1)S(1)}, bf16[2,256,256]{2,1,0:T(8,128)(2,1)}, u32[]{:S(2)}, u32[]{:S(2)}) collective-permute-start(bf16[2,256,256]{2,1,0:T(8,128)(2,1)S(1)} %get-tuple-element.33), channel_id=1, source_target_pairs={{0,6},{4,10},{8,14},{1,7},{5,11},{9,15},{16,22},{20,26},{24,30},{1... | collective-permute-start | bytes 786440 | tf_op jit(solution)/shard_map/ppermute | solution.py:34
  59.7 1.2 %maximum_bitcast_fusion = bf16[1,6,256,256]{3,2,1,0:T(8,128)(2,1)S(1)} fusion(bf16[2,256,256]{2,1,0:T(8,128)(2,1)} %collective-permute-done.2, bf16[2,256,256]{2,1,0:T(8,128)(2,1)} %collective-permute-done.1, bf16[2,256,256]{2,1,0:T(8,128)(2,1)} %collective-permute-done), kind=kLoop, calls=%fused_computation.22 | loop fusion | flops 786432 | bytes 1572864 | tf_op jit(solution)/shard_map/stack | solution.py:76
  60.9 6.9 %collective-permute-start.6 = (bf16[2,256,256]{2,1,0:T(8,128)(2,1)S(1)}, bf16[2,256,256]{2,1,0:T(8,128)(2,1)}, u32[]{:S(2)}, u32[]{:S(2)}) collective-permute-start(bf16[2,256,256]{2,1,0:T(8,128)(2,1)S(1)} %get-tuple-element.30), channel_id=1, source_target_pairs={{6,0},{10,4},{14,8},{7,1},{11,5},{15,9},{22,16},{26,20},{30,24},{2... | collective-permute-start | bytes 786440 | tf_op jit(solution)/shard_map/ppermute | solution.py:34
  67.8 2.0 %collective-permute-start.7 = (bf16[2,256,256]{2,1,0:T(8,128)(2,1)S(1)}, bf16[2,256,256]{2,1,0:T(8,128)(2,1)}, u32[]{:S(2)}, u32[]{:S(2)}) collective-permute-start(bf16[2,256,256]{2,1,0:T(8,128)(2,1)S(1)} %get-tuple-element.35), channel_id=1, source_target_pairs={{2,0},{6,4},{10,8},{14,12},{3,1},{7,5},{11,9},{15,13},{18,16},{22,... | collective-permute-start | bytes 786440 | tf_op jit(solution)/shard_map/ppermute | solution.py:34
  69.8 2.0 %collective-permute-start.8 = (bf16[2,256,256]{2,1,0:T(8,128)(2,1)S(1)}, bf16[2,256,256]{2,1,0:T(8,128)(2,1)}, u32[]{:S(2)}, u32[]{:S(2)}) collective-permute-start(bf16[2,256,256]{2,1,0:T(8,128)(2,1)S(1)} %get-tuple-element.34), channel_id=1, source_target_pairs={{2,4},{6,8},{10,12},{3,5},{7,9},{11,13},{18,20},{22,24},{26,28},{1... | collective-permute-start | bytes 786440 | tf_op jit(solution)/shard_map/ppermute | solution.py:34
  71.8 1.1 maximum_bitcast_fusion.1
  72.9 1.5 %multiply_bitcast_fusion = bf16[2,6,340,256]{3,2,1,0:T(8,128)(2,1)S(1)} fusion(bf16[1,6,256,256]{3,2,1,0:T(8,128)(2,1)S(1)} %maximum_bitcast_fusion.1, bf16[1,6,256,256]{3,2,1,0:T(8,128)(2,1)S(1)} %maximum_bitcast_fusion, bf16[2]{0:T(256)(128)(2,1)S(1)} %copy-done.8, bf16[4,256]{1,0:T(4,128)(2,1)} %select_convert_fusion.2, ...), kind=kOutput, calls=%fused_computation.7 | convolution fusion | flops 538345472 | bytes 3835908 | tf_op jit(solution)/shard_map/mp,jwpc->jwmc/dot_general | solution.py:77
  74.5 4.8 %gather_fusion = bf16[18,2,340,256]{3,2,1,0:T(8,128)(2,1)} fusion(bf16[2,6,340,256]{3,2,1,0:T(8,128)(2,1)S(1)} %multiply_bitcast_fusion, s32[1024]{0:T(1024)} %pad_clamp_fusion), kind=kCustom, calls=%fused_computation | custom fusion | bytes 12533832 | tf_op jit(solution)/shard_map/gather | solution.py:90
  79.3 1.5 %collective-permute-start.9 = (bf16[2,256,256]{2,1,0:T(8,128)(2,1)S(1)}, bf16[2,256,256]{2,1,0:T(8,128)(2,1)S(1)}, u32[]{:S(2)}, u32[]{:S(2)}) collective-permute-start(bf16[2,256,256]{2,1,0:T(8,128)(2,1)S(1)} %get-tuple-element.31), channel_id=1, source_target_pairs={{4,2},{8,6},{12,10},{5,3},{9,7},{13,11},{20,18},{24,22},{28,26},{2... | collective-permute-start | bytes 786440 | tf_op jit(solution)/shard_map/ppermute | solution.py:34
  80.8 5.9 %fusion.17 = f32[2,256,128]{2,1,0:T(8,128)S(1)} fusion(bf16[2,128,9,340]{1,0,3,2:T(2,128)(2,1)} %bitcast.151, bf16[2,9,2,340,256]{4,3,2,1,0:T(8,128)(2,1)} %bitcast.147, bf16[2,128]{1,0:T(2,128)(2,1)S(1)} %copy-done.2), kind=kOutput, calls=%fused_computation.19 | convolution fusion | flops 803009536 | bytes 8096256 | tf_op jit(solution)/shard_map/apkm,jakmc->japc/dot_general | solution.py:100
  86.7 0.1 copy.70
  86.9 2.6 %collective-permute-done.9 = bf16[2,256,256]{2,1,0:T(8,128)(2,1)S(1)} collective-permute-done((bf16[2,256,256]{2,1,0:T(8,128)(2,1)S(1)}, bf16[2,256,256]{2,1,0:T(8,128)(2,1)S(1)}, u32[]{:S(2)}, u32[]{:S(2)}) %collective-permute-start.9) | collective-permute-done | bytes 262176 | tf_op jit(solution)/shard_map/ppermute | solution.py:34
  89.5 1.5 %convert_add_fusion = f32[2,256,256]{2,1,0:T(8,128)S(1)} fusion(bf16[2,256,256]{2,1,0:T(8,128)(2,1)} %collective-permute-done.11, bf16[2,256,256]{2,1,0:T(8,128)(2,1)} %collective-permute-done.10, bf16[2,256,256]{2,1,0:T(8,128)(2,1)S(1)} %collective-permute-done.9, bf16[2,256,256]{2,1,0:T(8,128)(2,1)} %collective-permute-done.8, ...), kind=kLoop, calls=%fused_computation.24 | loop fusion | flops 1441792 | bytes 2097152 | tf_op jit(solution)/shard_map/add | solution.py:120
  91.0 0.1 fusion.25
  91.0 0.8 copy-done
  91.9 0.9 dynamic-slice_bitcast_fusion
  92.8 4.6 %fusion.10 = bf16[9,340,2,128]{3,1,0,2:T(8,128)(2,1)S(1)} fusion(f32[2,128]{1,0:T(2,128)S(1)} %convert_multiply_fusion, bf16[2,2,9,340,256]{4,3,0,2,1:T(8,128)(2,1)} %bitcast.148, bf16[2,128,256]{2,1,0:T(8,128)(2,1)S(1)} %dynamic-slice_bitcast_fusion), kind=kOutput, calls=%fused_computation.16 | convolution fusion | flops 803727360 | bytes 7965696 | tf_op jit(solution)/shard_map/jakmc,japc->kmap/dot_general | solution.py:92
  97.5 0.3 convert_element_type.86
  97.8 12.1 %copy.71 = bf16[1,2,128,3060]{2,1,3,0:T(2,128)(2,1)} copy(bf16[1,2,128,3060]{2,3,1,0:T(8,128)(2,1)S(1)} %bitcast.149) | data formatting | bytes 3133440
  (40 shorter events, 0.3 us)
Async XLA Ops:
  7.2 102.7 %reduce-scatter.2.cloned.1.call-start = ((), (), s32[]{:S(2)}) async-start(), calls=%async_computation.1 | async-start | bytes 786432 | tf_op jit(solution)/shard_map/reduce_scatter | solution.py:124
  10.8 43.8 %collective-permute-start = (bf16[2,256,256]{2,1,0:T(8,128)(2,1)}, bf16[2,256,256]{2,1,0:T(8,128)(2,1)}, u32[]{:S(2)}, u32[]{:S(2)}) collective-permute-start(bf16[2,256,256]{2,1,0:T(8,128)(2,1)} %bitcast.2), channel_id=1, source_target_pairs={{0,6},{4,10},{8,14},{1,7},{5,11},{9,15},{16,22},{20,26},{24,30},{1... | collective-permute-start | bytes 786440 | tf_op jit(solution)/shard_map/ppermute | solution.py:34
  12.1 45.1 %collective-permute-start.1 = (bf16[2,256,256]{2,1,0:T(8,128)(2,1)}, bf16[2,256,256]{2,1,0:T(8,128)(2,1)}, u32[]{:S(2)}, u32[]{:S(2)}) collective-permute-start(bf16[2,256,256]{2,1,0:T(8,128)(2,1)} %bitcast.2), channel_id=1, source_target_pairs={{0,2},{4,6},{8,10},{12,14},{1,3},{5,7},{9,11},{13,15},{16,18},{20,... | collective-permute-start | bytes 786440 | tf_op jit(solution)/shard_map/ppermute | solution.py:34
  13.4 45.0 %collective-permute-start.2 = (bf16[2,256,256]{2,1,0:T(8,128)(2,1)}, bf16[2,256,256]{2,1,0:T(8,128)(2,1)}, u32[]{:S(2)}, u32[]{:S(2)}) collective-permute-start(bf16[2,256,256]{2,1,0:T(8,128)(2,1)} %bitcast.2), channel_id=1, source_target_pairs={{4,2},{8,6},{12,10},{5,3},{9,7},{13,11},{20,18},{24,22},{28,26},{2... | collective-permute-start | bytes 786440 | tf_op jit(solution)/shard_map/ppermute | solution.py:34
  14.7 46.3 %collective-permute-start.3 = (bf16[2,256,256]{2,1,0:T(8,128)(2,1)}, bf16[2,256,256]{2,1,0:T(8,128)(2,1)}, u32[]{:S(2)}, u32[]{:S(2)}) collective-permute-start(bf16[2,256,256]{2,1,0:T(8,128)(2,1)} %bitcast.2), channel_id=1, source_target_pairs={{2,4},{6,8},{10,12},{3,5},{7,9},{11,13},{18,20},{22,24},{26,28},{1... | collective-permute-start | bytes 786440 | tf_op jit(solution)/shard_map/ppermute | solution.py:34
  24.0 43.8 %collective-permute-start.4 = (bf16[2,256,256]{2,1,0:T(8,128)(2,1)}, bf16[2,256,256]{2,1,0:T(8,128)(2,1)}, u32[]{:S(2)}, u32[]{:S(2)}) collective-permute-start(bf16[2,256,256]{2,1,0:T(8,128)(2,1)} %bitcast.2), channel_id=1, source_target_pairs={{2,0},{6,4},{10,8},{14,12},{3,1},{7,5},{11,9},{15,13},{18,16},{22,... | collective-permute-start | bytes 786440 | tf_op jit(solution)/shard_map/ppermute | solution.py:34
  26.7 0.6 copy-start.1
  29.7 2.3 %copy-start.4 = (s32[2,9]{1,0:T(2,128)S(1)}, s32[2,9]{1,0:T(2,128)}, u32[]{:S(2)}) copy-start(s32[2,9]{1,0:T(2,128)} %param.6) | copy-start | bytes 220
  43.1 4.3 %copy-start.6 = (s32[1,2]{1,0:T(1,128)S(1)}, s32[1,2]{1,0:T(1,128)}, u32[]{:S(2)}) copy-start(s32[1,2]{1,0:T(1,128)} %param.7) | copy-start | bytes 28
  52.1 3.7 %copy-start.7 = (s32[1,2]{1,0:T(1,128)S(1)}, s32[1,2]{1,0:T(1,128)}, u32[]{:S(2)}) copy-start(s32[1,2]{1,0:T(1,128)} %param.7) | copy-start | bytes 28
  52.2 4.3 %copy-start.5 = (s32[2,9]{1,0:T(2,128)S(1)}, s32[2,9]{1,0:T(2,128)}, u32[]{:S(2)}) copy-start(s32[2,9]{1,0:T(2,128)} %get-tuple-element.10) | copy-start | bytes 220
  54.6 15.2 %collective-permute-start.5 = (bf16[2,256,256]{2,1,0:T(8,128)(2,1)}, bf16[2,256,256]{2,1,0:T(8,128)(2,1)S(1)}, u32[]{:S(2)}, u32[]{:S(2)}) collective-permute-start(bf16[2,256,256]{2,1,0:T(8,128)(2,1)} %bitcast.2), channel_id=1, source_target_pairs={{6,0},{10,4},{14,8},{7,1},{11,5},{15,9},{22,16},{26,20},{30,24},{2... | collective-permute-start | bytes 786440 | tf_op jit(solution)/shard_map/ppermute | solution.py:34
  56.5 16.4 %copy-start.8 = (bf16[2]{0:T(256)(128)(2,1)S(1)}, bf16[2]{0:T(256)(128)(2,1)}, u32[]{:S(2)}) copy-start(bf16[2]{0:T(256)(128)(2,1)} %convert_bitcast_fusion) | copy-start | bytes 16
  57.1 22.2 %collective-permute-start.10 = (bf16[2,256,256]{2,1,0:T(8,128)(2,1)}, bf16[2,256,256]{2,1,0:T(8,128)(2,1)}, u32[]{:S(2)}, u32[]{:S(2)}) collective-permute-start(bf16[2,256,256]{2,1,0:T(8,128)(2,1)} %get-tuple-element.32), channel_id=1, source_target_pairs={{0,2},{4,6},{8,10},{12,14},{1,3},{5,7},{9,11},{13,15},{16,18},{20,... | collective-permute-start | bytes 786440 | tf_op jit(solution)/shard_map/ppermute | solution.py:34
  58.4 28.4 %collective-permute-start.11 = (bf16[2,256,256]{2,1,0:T(8,128)(2,1)S(1)}, bf16[2,256,256]{2,1,0:T(8,128)(2,1)}, u32[]{:S(2)}, u32[]{:S(2)}) collective-permute-start(bf16[2,256,256]{2,1,0:T(8,128)(2,1)S(1)} %get-tuple-element.33), channel_id=1, source_target_pairs={{0,6},{4,10},{8,14},{1,7},{5,11},{9,15},{16,22},{20,26},{24,30},{1... | collective-permute-start | bytes 786440 | tf_op jit(solution)/shard_map/ppermute | solution.py:34
  60.9 25.9 %collective-permute-start.6 = (bf16[2,256,256]{2,1,0:T(8,128)(2,1)S(1)}, bf16[2,256,256]{2,1,0:T(8,128)(2,1)}, u32[]{:S(2)}, u32[]{:S(2)}) collective-permute-start(bf16[2,256,256]{2,1,0:T(8,128)(2,1)S(1)} %get-tuple-element.30), channel_id=1, source_target_pairs={{6,0},{10,4},{14,8},{7,1},{11,5},{15,9},{22,16},{26,20},{30,24},{2... | collective-permute-start | bytes 786440 | tf_op jit(solution)/shard_map/ppermute | solution.py:34
  67.8 19.0 %collective-permute-start.7 = (bf16[2,256,256]{2,1,0:T(8,128)(2,1)S(1)}, bf16[2,256,256]{2,1,0:T(8,128)(2,1)}, u32[]{:S(2)}, u32[]{:S(2)}) collective-permute-start(bf16[2,256,256]{2,1,0:T(8,128)(2,1)S(1)} %get-tuple-element.35), channel_id=1, source_target_pairs={{2,0},{6,4},{10,8},{14,12},{3,1},{7,5},{11,9},{15,13},{18,16},{22,... | collective-permute-start | bytes 786440 | tf_op jit(solution)/shard_map/ppermute | solution.py:34
  69.8 17.1 %collective-permute-start.8 = (bf16[2,256,256]{2,1,0:T(8,128)(2,1)S(1)}, bf16[2,256,256]{2,1,0:T(8,128)(2,1)}, u32[]{:S(2)}, u32[]{:S(2)}) collective-permute-start(bf16[2,256,256]{2,1,0:T(8,128)(2,1)S(1)} %get-tuple-element.34), channel_id=1, source_target_pairs={{2,4},{6,8},{10,12},{3,5},{7,9},{11,13},{18,20},{22,24},{26,28},{1... | collective-permute-start | bytes 786440 | tf_op jit(solution)/shard_map/ppermute | solution.py:34
  74.5 6.3 %copy-start.2 = (bf16[2,128]{1,0:T(2,128)(2,1)S(1)}, bf16[2,128]{1,0:T(2,128)(2,1)}, u32[]{:S(2)}) copy-start(bf16[2,128]{1,0:T(2,128)(2,1)} %copy-done.1) | copy-start | bytes 1540
  79.3 10.2 %collective-permute-start.9 = (bf16[2,256,256]{2,1,0:T(8,128)(2,1)S(1)}, bf16[2,256,256]{2,1,0:T(8,128)(2,1)S(1)}, u32[]{:S(2)}, u32[]{:S(2)}) collective-permute-start(bf16[2,256,256]{2,1,0:T(8,128)(2,1)S(1)} %get-tuple-element.31), channel_id=1, source_target_pairs={{4,2},{8,6},{12,10},{5,3},{9,7},{13,11},{20,18},{24,22},{28,26},{2... | collective-permute-start | bytes 786440 | tf_op jit(solution)/shard_map/ppermute | solution.py:34
  86.7 5.2 %copy-start.3 = (s32[2,256]{1,0:T(2,128)S(1)}, s32[2,256]{1,0:T(2,128)}, u32[]{:S(2)}) copy-start(s32[2,256]{1,0:T(2,128)} %param.8) | copy-start | bytes 6148
  91.0 0.8 copy-start
Sparse Core Ops, SparseCore 0:
  92.0 7.8 reduce-scatter.1

commit v4 on v2

--- a/solution.py
+++ b/solution.py
@@ -77,11 +77,13 @@
     slot_ids = neighbours - (lax.axis_index("tile") * tile_count - tile_count)
     chosen = pyramid[:, slot_ids]
     queries2 = jnp.broadcast_to(queries[None], (2,) + queries.shape)
-    scores = jnp.einsum(
-        "jakmc,japc->kmap", chosen, queries2, preferred_element_type=jnp.float32
-    )
-    summed = scores * scale[None, None]
-    volume = summed.reshape(NEIGHBOURS * LEVELS, tile_count, half_rows).astype(jnp.bfloat16)
+    per_tile = []
+    for a in range(tile_count):
+        tile_scores = jnp.einsum(
+            "jkmc,jpc->kmp", chosen[:, a], queries2[:, a], preferred_element_type=jnp.float32
+        )
+        per_tile.append(tile_scores.reshape(NEIGHBOURS * LEVELS, half_rows) * scale[a][None])
+    volume = jnp.stack(per_tile, 1).astype(jnp.bfloat16)
     volume = jnp.transpose(volume, (1, 2, 0))[None]
     upstream = cotangent[0].reshape(tile_count, half_rows, NEIGHBOURS, LEVELS)
     upstream = upstream * valid_local.astype(jnp.bfloat16)[:, :, None, None]

time: 109 us -> 122 us (1.12)
  local copies, waits for them, and re-layouts: 31.3 us -> 44.6 us
    dot_general x0 -> x3, local copies, waits for them, and re-layouts: none -> 10.3 us  [local(): jnp.einsum('jkmc,jpc->kmp', chosen[:, a], queries2[:, a], preferred_eleme...]
    gather x1 -> x2, local copies, waits for them, and re-layouts: 4.65 us -> 7.85 us  [local(): chosen = pyramid[:, slot_ids]]
    dot_general x1 -> x2, matrix products: 4.64 us -> 3.99 us  [local(): jnp.einsum('jkmc,jpc->kmp', chosen[:, a], queries2[:, a], preferred_eleme...]
    unnamed x9 -> x13, local copies, waits for them, and re-layouts: 12.9 us -> 12.9 us
  transfers between devices with their start and end apart: 9 -> 9, of which waited for: 2 -> 2; matrix products, arithmetic and copies ran while one was open for 42% -> 46% of each run, Pallas kernels for 0% -> 0%
where the time goes in v4:
time: 122 us
  local copies, waits for them, and re-layouts  44.6 us (37%)
  starting transfers between devices  23.9 us (20%)
  between operations  14.4 us (12%)
  matrix products  14.3 us (12%)
  other arithmetic  13.3 us (11%)
  waiting for transfers between devices  7.29 us (6%)
  blocking collectives  3.93 us (3%)
    ppermute x8, starting transfers between devices, shift(): return lax.ppermute(x, axis, pairs)  23.9 us
    unnamed x13, local copies, waits for them, and re-layouts  12.9 us
    dot_general x3, local copies, waits for them, and re-layouts, local(): jnp.einsum('jkmc,jpc->kmp', chosen[:, a], queries2[:, a], preferred_eleme...  10.3 us
    gather x2, local copies, waits for them, and re-layouts, local(): chosen = pyramid[:, slot_ids]  7.85 us
    ppermute x8, waiting for transfers between devices, shift(): return lax.ppermute(x, axis, pairs)  7.27 us
    dot_general x1, matrix products, local(): jnp.einsum('apkm,jakmc->japc', upstream, chosen, preferred_element_type=j...  6.06 us
    reshape x2, local copies, waits for them, and re-layouts, pool_back(): part = part.reshape(lead, PIXELS, chans)  5.89 us
    add x1, other arithmetic, local(): cells = term if cells is None else cells + term  5.22 us
  transfers between devices with their start and end apart: 9, of which 2 were waited for; matrix products, arithmetic and copies ran while one was open for 46% of the time, Pallas kernels for 0%

profile of v4, /device:TPU:0, one launch (start us, length us, event | category | flops | bytes accessed | tf_op | source)
XLA Modules:
  0.0 121.6 jit_solution(8176530539817420282)
XLA Ops:
  7.2 0.0 reduce-scatter.2.cloned.1.call-start
  7.2 3.9 %all_gather.3 = bf16[1,2,256,256]{3,2,1,0:T(8,128)(2,1)} all-gather(bf16[1,2,256,128]{3,2,1,0:T(8,128)(2,1)} %param.5), channel_id=1, replica_groups=mesh['clip'=2,'tile'=4,'frame'=2,'chan'=2] {'chan'}, dimensions={3}, use_global_device_ids=true | all-gather | bytes 393216 | tf_op jit(solution)/shard_map/all_gather | solution.py:58
  11.1 5.2 %collective-permute-start = (bf16[2,256,256]{2,1,0:T(8,128)(2,1)}, bf16[2,256,256]{2,1,0:T(8,128)(2,1)}, u32[]{:S(2)}, u32[]{:S(2)}) collective-permute-start(bf16[2,256,256]{2,1,0:T(8,128)(2,1)} %bitcast), channel_id=1, source_target_pairs={{0,2},{1,3},{4,6},{5,7},{8,10},{9,11},{12,14},{13,15},{16,18},{17,... | collective-permute-start | bytes 786440 | tf_op jit(solution)/shard_map/ppermute | solution.py:22
  16.4 1.3 %collective-permute-start.1 = (bf16[2,256,256]{2,1,0:T(8,128)(2,1)}, bf16[2,256,256]{2,1,0:T(8,128)(2,1)}, u32[]{:S(2)}, u32[]{:S(2)}) collective-permute-start(bf16[2,256,256]{2,1,0:T(8,128)(2,1)} %bitcast), channel_id=1, source_target_pairs={{2,0},{3,1},{6,4},{7,5},{10,8},{11,9},{14,12},{15,13},{18,16},{19,... | collective-permute-start | bytes 786440 | tf_op jit(solution)/shard_map/ppermute | solution.py:22
  17.6 0.7 fusion.46
  18.3 2.4 %fusion.20 = f32[2,9,340,256]{3,2,1,0:T(8,128)S(1)} fusion(bf16[2,128,9,340]{1,0,3,2:T(2,128)(2,1)} %bitcast.171, bf16[2,128]{1,0:T(2,128)(2,1)S(1)} %fusion.46, bf16[1,2,256,256]{3,2,1,0:T(8,128)(2,1)} %all_gather.3, s32[]{:T(128)S(6)} %select_n.113), kind=kOutput, calls=%fused_computation.29 | convolution fusion | flops 401863680 | bytes 7965188 | tf_op jit(solution)/shard_map/apkm,apc->akmc/dot_general | solution.py:94
  20.7 0.0 copy-start.4
  20.7 2.3 %slice_bitcast_fusion.19 = (f32[340,256]{1,0:T(8,128)S(1)}, f32[340,256]{1,0:T(8,128)S(1)}, f32[340,256]{1,0:T(8,128)S(1)}, f32[340,256]{1,0:T(8,128)S(1)}, f32[...) fusion(f32[2,9,340,256]{3,2,1,0:T(8,128)S(1)} %fusion.20), kind=kLoop, calls=%fused_computation.58 | loop fusion | bytes 12533760 | tf_op jit(solution)/shard_map/mul | solution.py:101
  23.0 0.1 fusion.39
  23.1 5.2 %multiply_add_fusion = f32[6,340,256]{2,1,0:T(8,128)S(1)} fusion(f32[340,256]{1,0:T(8,128)S(1)} %get-tuple-element.17, f32[6]{0:T(128)S(1)} %get-tuple-element.43, f32[340,256]{1,0:T(8,128)S(1)} %get-tuple-element.18, f32[6]{0:T(128)S(1)} %get-tuple-element.44, f32[340,256]{1,0:T(8,128)S(1)} %get-tuple-element.19, f32[6]{0:T(128)S(1)} %get-tuple-element.45, ...), kind=kLoop, calls=%fused_computation.12 | loop fusion | flops 18278400 | bytes 8356272 | tf_op jit(solution)/shard_map/add | solution.py:102
  28.4 1.9 %broadcast_in_dim.62 = f32[6,8,2,8,2,256]{5,4,3,2,1,0:T(2,128)} broadcast(f32[6,8,8,256]{3,2,1,0:T(8,128)S(1)} %fusion.27), dimensions={0,1,3,5} | broadcast | bytes 1966080 | tf_op jit(solution)/shard_map/broadcast_in_dim | solution.py:48
  30.3 3.1 %reshape.186 = f32[6,256,256]{2,1,0:T(8,128)} reshape(f32[6,8,2,8,2,256]{5,4,3,2,1,0:T(2,128)} %broadcast_in_dim.62) | data formatting | bytes 3145728 | tf_op jit(solution)/shard_map/reshape | solution.py:49
  33.5 1.6 %broadcast_in_dim.64 = f32[6,4,4,4,4,256]{5,4,3,2,1,0:T(4,128)} broadcast(f32[6,4,4,256]{3,2,1,0:T(4,128)S(1)} %broadcast_in_dim.63), dimensions={0,1,3,5} | broadcast | bytes 1671168 | tf_op jit(solution)/shard_map/broadcast_in_dim | solution.py:48
  35.1 2.7 %reshape.187 = f32[6,256,256]{2,1,0:T(8,128)} reshape(f32[6,4,4,4,4,256]{5,4,3,2,1,0:T(4,128)} %broadcast_in_dim.64) | data formatting | bytes 3145728 | tf_op jit(solution)/shard_map/reshape | solution.py:49
  37.9 0.0 copy-start.3
  37.9 0.0 copy-start.5
  37.9 3.4 %fusion.48 = (bf16[6,256,256]{2,1,0:T(8,128)(2,1)S(1)}, f32[6,256,256]{2,1,0:T(8,128)}) fusion(f32[6,2,2,256]{3,2,1,0:T(2,128)S(1)} %broadcast_in_dim.65, f32[6,256,256]{2,1,0:T(8,128)} %reshape.187, f32[6,256,256]{2,1,0:T(8,128)} %reshape.186, f32[6,340,256]{2,1,0:T(8,128)S(1)} %multiply_add_fusion), kind=kLoop, calls=%fused_computation.151 | loop fusion | flops 1572864 | bytes 7102464 | tf_op jit(solution)/shard_map/convert.1
  41.3 1.3 %collective-permute-start.4 = (bf16[2,256,256]{2,1,0:T(8,128)(2,1)S(1)}, bf16[2,256,256]{2,1,0:T(8,128)(2,1)S(1)}, u32[]{:S(2)}, u32[]{:S(2)}) collective-permute-start(bf16[2,256,256]{2,1,0:T(8,128)(2,1)S(1)} %get-tuple-element.38), channel_id=1, source_target_pairs={{4,0},{8,4},{12,8},{5,1},{9,5},{13,9},{6,2},{10,6},{14,10},{7,3},{... | collective-permute-start | bytes 786440 | tf_op jit(solution)/shard_map/ppermute | solution.py:22
  42.6 4.6 %collective-permute-start.5 = (bf16[2,256,256]{2,1,0:T(8,128)(2,1)S(1)}, bf16[2,256,256]{2,1,0:T(8,128)(2,1)S(1)}, u32[]{:S(2)}, u32[]{:S(2)}) collective-permute-start(bf16[2,256,256]{2,1,0:T(8,128)(2,1)S(1)} %get-tuple-element.39), channel_id=1, source_target_pairs={{0,4},{4,8},{8,12},{1,5},{5,9},{9,13},{2,6},{6,10},{10,14},{3,7},{... | collective-permute-start | bytes 786440 | tf_op jit(solution)/shard_map/ppermute | solution.py:22
  47.3 0.6 fusion.51
  47.9 0.1 reshape.191
  48.0 0.9 dynamic-slice_bitcast_fusion.1
  48.9 0.0 collective-permute-done
  48.9 1.1 pad_maximum_fusion
  50.0 3.5 %collective-permute-start.2 = (bf16[2,2,256,256]{3,2,1,0:T(8,128)(2,1)S(1)}, bf16[2,2,256,256]{3,2,1,0:T(8,128)(2,1)S(1)}, u32[]{:S(2)}, u32[]{:S(2)}) collective-permute-start(bf16[2,2,256,256]{3,2,1,0:T(8,128)(2,1)S(1)} %pad_maximum_fusion), channel_id=1, source_target_pairs={{0,4},{4,8},{8,12},{1,5},{5,9},{9,13},{2,6},{6,10},{10,14},{3,7},{... | collective-permute-start | bytes 1572872 | tf_op jit(solution)/shard_map/ppermute | solution.py:22
  53.5 1.3 %collective-permute-start.3 = (bf16[2,2,256,256]{3,2,1,0:T(8,128)(2,1)S(1)}, bf16[2,2,256,256]{3,2,1,0:T(8,128)(2,1)S(1)}, u32[]{:S(2)}, u32[]{:S(2)}) collective-permute-start(bf16[2,2,256,256]{3,2,1,0:T(8,128)(2,1)S(1)} %pad_maximum_fusion), channel_id=1, source_target_pairs={{4,0},{8,4},{12,8},{5,1},{9,5},{13,9},{6,2},{10,6},{14,10},{7,3},{... | collective-permute-start | bytes 1572872 | tf_op jit(solution)/shard_map/ppermute | solution.py:22
  54.8 0.0 collective-permute-done.4
  54.8 2.5 %multiply_convert_fusion.1 = (bf16[2,256,256]{2,1,0:T(8,128)(2,1)S(1)}, bf16[2,256,256]{2,1,0:T(8,128)(2,1)S(1)}) fusion(f32[]{:T(128)} %bitcast.65, bf16[2,256,256]{2,1,0:T(8,128)(2,1)S(1)} %collective-permute-done.5, f32[6,256,256]{2,1,0:T(8,128)} %get-tuple-element.13, bf16[2,256,256]{2,1,0:T(8,128)(2,1)S(1)} %collective-permute-done.4, f32[]{:T(128)} %bitcast.66), kind=kLoop, calls=%fused_computation.38 | loop fusion | flops 1048576 | bytes 1572872 | tf_op jit(solution)/shard_map/convert_element_type | solution.py:113
  57.3 5.2 %collective-permute-start.6 = (bf16[2,256,256]{2,1,0:T(8,128)(2,1)S(1)}, bf16[2,256,256]{2,1,0:T(8,128)(2,1)S(1)}, u32[]{:S(2)}, u32[]{:S(2)}) collective-permute-start(bf16[2,256,256]{2,1,0:T(8,128)(2,1)S(1)} %get-tuple-element.36), channel_id=1, source_target_pairs={{0,2},{1,3},{4,6},{5,7},{8,10},{9,11},{12,14},{13,15},{16,18},{17,... | collective-permute-start | bytes 786440 | tf_op jit(solution)/shard_map/ppermute | solution.py:22
  62.5 1.5 %collective-permute-start.7 = (bf16[2,256,256]{2,1,0:T(8,128)(2,1)S(1)}, bf16[2,256,256]{2,1,0:T(8,128)(2,1)S(1)}, u32[]{:S(2)}, u32[]{:S(2)}) collective-permute-start(bf16[2,256,256]{2,1,0:T(8,128)(2,1)S(1)} %get-tuple-element.37), channel_id=1, source_target_pairs={{2,0},{3,1},{6,4},{7,5},{10,8},{11,9},{14,12},{15,13},{18,16},{19,... | collective-permute-start | bytes 786440 | tf_op jit(solution)/shard_map/ppermute | solution.py:22
  64.0 3.1 %collective-permute-done.6 = bf16[2,256,256]{2,1,0:T(8,128)(2,1)S(1)} collective-permute-done((bf16[2,256,256]{2,1,0:T(8,128)(2,1)S(1)}, bf16[2,256,256]{2,1,0:T(8,128)(2,1)S(1)}, u32[]{:S(2)}, u32[]{:S(2)}) %collective-permute-start.6) | collective-permute-done | bytes 262176 | tf_op jit(solution)/shard_map/ppermute | solution.py:22
  67.2 4.1 %collective-permute-done.7 = bf16[2,256,256]{2,1,0:T(8,128)(2,1)S(1)} collective-permute-done((bf16[2,256,256]{2,1,0:T(8,128)(2,1)S(1)}, bf16[2,256,256]{2,1,0:T(8,128)(2,1)S(1)}, u32[]{:S(2)}, u32[]{:S(2)}) %collective-permute-start.7) | collective-permute-done | bytes 262176 | tf_op jit(solution)/shard_map/ppermute | solution.py:22
  71.3 0.1 convert_add_fusion
  71.4 1.8 %multiply_bitcast_fusion = bf16[2,6,340,256]{3,2,1,0:T(8,128)(2,1)S(1)} fusion(bf16[2,2,256,256]{3,2,1,0:T(8,128)(2,1)S(1)} %collective-permute-done.3, bf16[1,2,256,256]{3,2,1,0:T(8,128)(2,1)} %bitcast.2, bf16[1,2,256,256]{3,2,1,0:T(8,128)(2,1)} %bitcast.1, bf16[2,2,256,256]{3,2,1,0:T(8,128)(2,1)S(1)} %collective-permute-done.2, ...), kind=kOutput, calls=%fused_computation.13 | convolution fusion | flops 539918336 | bytes 3835908 | tf_op jit(solution)/shard_map/mp,jwpc->jwmc/dot_general | solution.py:65
  73.2 4.7 %gather_fusion = bf16[18,2,340,256]{3,2,1,0:T(8,128)(2,1)} fusion(bf16[2,6,340,256]{3,2,1,0:T(8,128)(2,1)S(1)} %multiply_bitcast_fusion, s32[1024]{0:T(1024)S(1)} %pad_clamp_fusion), kind=kCustom, calls=%fused_computation | custom fusion | bytes 12533832 | tf_op jit(solution)/shard_map/gather | solution.py:78
  77.9 6.1 %fusion.21 = f32[2,256,128]{2,1,0:T(8,128)S(1)} fusion(bf16[2,128,9,340]{1,0,3,2:T(2,128)(2,1)} %bitcast.172, bf16[2,128]{1,0:T(2,128)(2,1)S(1)} %fusion.46, bf16[2,9,2,340,256]{4,3,2,1,0:T(8,128)(2,1)} %bitcast.168), kind=kOutput, calls=%fused_computation.30 | convolution fusion | flops 803009536 | bytes 8096256 | tf_op jit(solution)/shard_map/apkm,jakmc->japc/dot_general | solution.py:90
  84.0 3.1 %copy.80 = bf16[2,9,2,340,256]{4,3,1,2,0:T(8,128)(2,1)} copy(bf16[2,9,2,340,256]{4,3,2,1,0:T(8,128)(2,1)S(1)} %bitcast.169) | data formatting | bytes 12533760 | tf_op jit(solution)/shard_map/gather | solution.py:78
  87.1 0.1 copy.65
  87.3 0.1 fusion.28
  87.3 0.8 copy-done.1
  88.1 0.0 reduce-scatter.2.cloned.1.call-update
  88.1 5.0 %slice_bitcast_fusion.1 = (bf16[9,340,256,2]{2,1,0,3:T(8,128)(2,1)}, bf16[9,340,256,2]{2,1,0,3:T(8,128)(2,1)S(1)}) fusion(bf16[2,2,9,340,256]{4,3,2,0,1:T(8,128)(2,1)} %bitcast.170), kind=kLoop, calls=%fused_computation.11 | loop fusion | bytes 12533760 | tf_op jit(solution)/shard_map/jkmc,jpc->kmp/dot_general | solution.py:82
  93.1 3.5 %dot_general.25 = bf16[3060,256,2]{1,0,2:T(8,128)(2,1)} reshape(bf16[9,340,256,2]{2,1,0,3:T(8,128)(2,1)} %get-tuple-element.34) | data formatting | bytes 6266880 | tf_op jit(solution)/shard_map/jkmc,jpc->kmp/dot_general | solution.py:82
  96.6 1.9 %dot_general.28 = bf16[3060,256,2]{1,0,2:T(8,128)(2,1)} reshape(bf16[9,340,256,2]{2,1,0,3:T(8,128)(2,1)S(1)} %get-tuple-element.35) | data formatting | bytes 6266880 | tf_op jit(solution)/shard_map/jkmc,jpc->kmp/dot_general | solution.py:82
  98.5 3.0 %fusion.5 = bf16[3060,1,128]{2,0,1:T(8,128)(2,1)S(1)} fusion(bf16[3060,256,2]{1,0,2:T(8,128)(2,1)} %dot_general.25, f32[128]{0:T(128)S(1)} %get-tuple-element.60, bf16[128,256]{1,0:T(8,128)(2,1)S(1)} %get-tuple-element.40), kind=kOutput, calls=%fused_computation.9 | convolution fusion | flops 401863680 | bytes 3982848 | tf_op jit(solution)/shard_map/jkmc,jpc->kmp/dot_general | solution.py:82
  101.5 1.0 fusion.4
  102.5 0.1 maximum_bitcast_fusion
  102.6 12.1 %copy.66 = bf16[1,2,128,3060]{2,1,3,0:T(2,128)(2,1)} copy(bf16[1,2,128,3060]{2,3,1,0:T(8,128)(2,1)S(1)} %maximum_bitcast_fusion) | data formatting | bytes 3133440
  (32 shorter events, 0.3 us)
Async XLA Ops:
  7.2 107.6 %reduce-scatter.2.cloned.1.call-start = ((), (), s32[]{:S(2)}) async-start(), calls=%async_computation.1 | async-start | bytes 786432 | tf_op jit(solution)/shard_map/reduce_scatter | solution.py:118
  11.1 37.7 %collective-permute-start = (bf16[2,256,256]{2,1,0:T(8,128)(2,1)}, bf16[2,256,256]{2,1,0:T(8,128)(2,1)}, u32[]{:S(2)}, u32[]{:S(2)}) collective-permute-start(bf16[2,256,256]{2,1,0:T(8,128)(2,1)} %bitcast), channel_id=1, source_target_pairs={{0,2},{1,3},{4,6},{5,7},{8,10},{9,11},{12,14},{13,15},{16,18},{17,... | collective-permute-start | bytes 786440 | tf_op jit(solution)/shard_map/ppermute | solution.py:22
  16.4 32.5 %collective-permute-start.1 = (bf16[2,256,256]{2,1,0:T(8,128)(2,1)}, bf16[2,256,256]{2,1,0:T(8,128)(2,1)}, u32[]{:S(2)}, u32[]{:S(2)}) collective-permute-start(bf16[2,256,256]{2,1,0:T(8,128)(2,1)} %bitcast), channel_id=1, source_target_pairs={{2,0},{3,1},{6,4},{7,5},{10,8},{11,9},{14,12},{15,13},{18,16},{19,... | collective-permute-start | bytes 786440 | tf_op jit(solution)/shard_map/ppermute | solution.py:22
  20.7 2.3 %copy-start.4 = (s32[2,9]{1,0:T(2,128)S(1)}, s32[2,9]{1,0:T(2,128)}, u32[]{:S(2)}) copy-start(s32[2,9]{1,0:T(2,128)} %param.6) | copy-start | bytes 220
  37.9 9.3 %copy-start.3 = (s32[2,256]{1,0:T(2,128)S(1)}, s32[2,256]{1,0:T(2,128)}, u32[]{:S(2)}) copy-start(s32[2,256]{1,0:T(2,128)} %param.8) | copy-start | bytes 6148
  37.9 9.3 %copy-start.5 = (s32[1,2]{1,0:T(1,128)S(1)}, s32[1,2]{1,0:T(1,128)}, u32[]{:S(2)}) copy-start(s32[1,2]{1,0:T(1,128)} %param.7) | copy-start | bytes 28
  41.3 13.5 %collective-permute-start.4 = (bf16[2,256,256]{2,1,0:T(8,128)(2,1)S(1)}, bf16[2,256,256]{2,1,0:T(8,128)(2,1)S(1)}, u32[]{:S(2)}, u32[]{:S(2)}) collective-permute-start(bf16[2,256,256]{2,1,0:T(8,128)(2,1)S(1)} %get-tuple-element.38), channel_id=1, source_target_pairs={{4,0},{8,4},{12,8},{5,1},{9,5},{13,9},{6,2},{10,6},{14,10},{7,3},{... | collective-permute-start | bytes 786440 | tf_op jit(solution)/shard_map/ppermute | solution.py:22
  42.6 12.2 %collective-permute-start.5 = (bf16[2,256,256]{2,1,0:T(8,128)(2,1)S(1)}, bf16[2,256,256]{2,1,0:T(8,128)(2,1)S(1)}, u32[]{:S(2)}, u32[]{:S(2)}) collective-permute-start(bf16[2,256,256]{2,1,0:T(8,128)(2,1)S(1)} %get-tuple-element.39), channel_id=1, source_target_pairs={{0,4},{4,8},{8,12},{1,5},{5,9},{9,13},{2,6},{6,10},{10,14},{3,7},{... | collective-permute-start | bytes 786440 | tf_op jit(solution)/shard_map/ppermute | solution.py:22
  50.0 21.4 %collective-permute-start.2 = (bf16[2,2,256,256]{3,2,1,0:T(8,128)(2,1)S(1)}, bf16[2,2,256,256]{3,2,1,0:T(8,128)(2,1)S(1)}, u32[]{:S(2)}, u32[]{:S(2)}) collective-permute-start(bf16[2,2,256,256]{3,2,1,0:T(8,128)(2,1)S(1)} %pad_maximum_fusion), channel_id=1, source_target_pairs={{0,4},{4,8},{8,12},{1,5},{5,9},{9,13},{2,6},{6,10},{10,14},{3,7},{... | collective-permute-start | bytes 1572872 | tf_op jit(solution)/shard_map/ppermute | solution.py:22
  53.5 17.9 %collective-permute-start.3 = (bf16[2,2,256,256]{3,2,1,0:T(8,128)(2,1)S(1)}, bf16[2,2,256,256]{3,2,1,0:T(8,128)(2,1)S(1)}, u32[]{:S(2)}, u32[]{:S(2)}) collective-permute-start(bf16[2,2,256,256]{3,2,1,0:T(8,128)(2,1)S(1)} %pad_maximum_fusion), channel_id=1, source_target_pairs={{4,0},{8,4},{12,8},{5,1},{9,5},{13,9},{6,2},{10,6},{14,10},{7,3},{... | collective-permute-start | bytes 1572872 | tf_op jit(solution)/shard_map/ppermute | solution.py:22
  57.3 9.9 %collective-permute-start.6 = (bf16[2,256,256]{2,1,0:T(8,128)(2,1)S(1)}, bf16[2,256,256]{2,1,0:T(8,128)(2,1)S(1)}, u32[]{:S(2)}, u32[]{:S(2)}) collective-permute-start(bf16[2,256,256]{2,1,0:T(8,128)(2,1)S(1)} %get-tuple-element.36), channel_id=1, source_target_pairs={{0,2},{1,3},{4,6},{5,7},{8,10},{9,11},{12,14},{13,15},{16,18},{17,... | collective-permute-start | bytes 786440 | tf_op jit(solution)/shard_map/ppermute | solution.py:22
  62.5 8.8 %collective-permute-start.7 = (bf16[2,256,256]{2,1,0:T(8,128)(2,1)S(1)}, bf16[2,256,256]{2,1,0:T(8,128)(2,1)S(1)}, u32[]{:S(2)}, u32[]{:S(2)}) collective-permute-start(bf16[2,256,256]{2,1,0:T(8,128)(2,1)S(1)} %get-tuple-element.37), channel_id=1, source_target_pairs={{2,0},{3,1},{6,4},{7,5},{10,8},{11,9},{14,12},{15,13},{18,16},{19,... | collective-permute-start | bytes 786440 | tf_op jit(solution)/shard_map/ppermute | solution.py:22
  77.9 6.1 %copy-start = (bf16[18,2,340,256]{3,2,1,0:T(8,128)(2,1)S(1)}, bf16[18,2,340,256]{3,2,1,0:T(8,128)(2,1)}, u32[]{:S(2)}) copy-start(bf16[18,2,340,256]{3,2,1,0:T(8,128)(2,1)} %gather_fusion) | copy-start | bytes 18800644
  87.3 0.8 copy-start.1
  98.5 3.0 %copy-start.2 = (bf16[3060,256,2]{1,0,2:T(8,128)(2,1)S(1)}, bf16[3060,256,2]{1,0,2:T(8,128)(2,1)}, u32[]{:S(2)}) copy-start(bf16[3060,256,2]{1,0,2:T(8,128)(2,1)} %dot_general.28) | copy-start | bytes 9400324
Sparse Core Ops, SparseCore 0:
  88.3 7.9 reduce-scatter.1

commit v5 on v2

--- a/solution.py
+++ b/solution.py
@@ -83,13 +83,14 @@
     summed = scores * scale[None, None]
     volume = summed.reshape(NEIGHBOURS * LEVELS, tile_count, half_rows).astype(jnp.bfloat16)
     volume = jnp.transpose(volume, (1, 2, 0))[None]
-    upstream = cotangent[0].reshape(tile_count, half_rows, NEIGHBOURS, LEVELS)
-    upstream = upstream * valid_local.astype(jnp.bfloat16)[:, :, None, None]
+    upstream = cotangent[0] * valid_local.astype(jnp.bfloat16)[:, :, None]
+    flat_chosen = chosen.reshape(2, tile_count, NEIGHBOURS * LEVELS, chosen.shape[-1])
     partial_query = jnp.einsum(
-        "apkm,jakmc->japc", upstream, chosen, preferred_element_type=jnp.float32
+        "apn,janc->japc", upstream, flat_chosen, preferred_element_type=jnp.float32
     )
     query_grad = jnp.sum(partial_query, axis=0) * (1.0 / math.sqrt(CHANNELS))
-    base_grad = jnp.einsum("apkm,apc->akmc", upstream, queries, preferred_element_type=jnp.float32)
+    flat_grad = jnp.einsum("apn,apc->anc", upstream, queries, preferred_element_type=jnp.float32)
+    base_grad = flat_grad.reshape(tile_count, NEIGHBOURS, LEVELS, flat_grad.shape[-1])
     member = (
         slot_ids[:, :, None] == jnp.arange(3 * tile_count, dtype=jnp.int32)[None, None, :]
     ).astype(jnp.float32)

time: 109 us -> 135 us (1.24)
  local copies, waits for them, and re-layouts: 31.3 us -> 51.1 us
  other arithmetic: 13.2 us -> 18.8 us
    reshape x0 -> x2, local copies, waits for them, and re-layouts: none -> 11.1 us  [the longest x1 6.26 us: local(): chosen.reshape(2, tile_count, NEIGHBOURS * LEVELS, chosen.shape[-1])]
    gather x1 -> x2, local copies, waits for them, and re-layouts: 4.65 us -> 10.6 us  [local(): chosen = pyramid[:, slot_ids]]
    mul x0 -> x2, other arithmetic: none -> 5.46 us  [local(): upstream = cotangent[0] * valid_local.astype(jnp.bfloat16)[:, :, None]]
    mul x2, local copies, waits for them, and re-layouts: 2.28 us -> 5.07 us  [local(): term = member[a, k][:, None, None] * base_grad[a, k][None]]
    unnamed x9 -> x17, local copies, waits for them, and re-layouts: 12.9 us -> 12.9 us
  transfers between devices with their start and end apart: 9 -> 9, of which waited for: 2 -> 2; matrix products, arithmetic and copies ran while one was open for 42% -> 45% of each run, Pallas kernels for 0% -> 0%
where the time goes in v5:
time: 135 us; the launch traced here: 134 us
  local copies, waits for them, and re-layouts  51.1 us (38%)
  starting transfers between devices  23.9 us (18%)
  other arithmetic  18.8 us (14%)
  matrix products  14.9 us (11%)
  between operations  14.4 us (11%)
  waiting for transfers between devices  7.29 us (5%)
  blocking collectives  3.92 us (3%)
    ppermute x8, starting transfers between devices, shift(): return lax.ppermute(x, axis, pairs)  23.9 us
    unnamed x17, local copies, waits for them, and re-layouts  12.9 us
    gather x2, local copies, waits for them, and re-layouts, local(): chosen = pyramid[:, slot_ids]  10.6 us
    ppermute x8, waiting for transfers between devices, shift(): return lax.ppermute(x, axis, pairs)  7.28 us
    reshape x1, local copies, waits for them, and re-layouts, local(): chosen.reshape(2, tile_count, NEIGHBOURS * LEVELS, chosen.shape[-1])  6.26 us
    reshape x2, local copies, waits for them, and re-layouts, pool_back(): part = part.reshape(lead, PIXELS, chans)  5.9 us
    mul x2, other arithmetic, local(): upstream = cotangent[0] * valid_local.astype(jnp.bfloat16)[:, :, None]  5.46 us
    add x1, other arithmetic, local(): cells = term if cells is None else cells + term  5.22 us
  transfers between devices with their start and end apart: 9, of which 2 were waited for; matrix products, arithmetic and copies ran while one was open for 45% of the time, Pallas kernels for 0%

profile of v5, /device:TPU:0, one launch (start us, length us, event | category | flops | bytes accessed | tf_op | source)
XLA Modules:
  0.0 134.3 jit_solution(3444970234117187123)
XLA Ops:
  7.2 0.0 reduce-scatter.2.cloned.1.call-start
  7.2 3.9 %all_gather.3 = bf16[1,2,256,256]{3,2,1,0:T(8,128)(2,1)} all-gather(bf16[1,2,256,128]{3,2,1,0:T(8,128)(2,1)} %param.5), channel_id=1, replica_groups=mesh['clip'=2,'tile'=4,'frame'=2,'chan'=2] {'chan'}, dimensions={3}, use_global_device_ids=true | all-gather | bytes 393216 | tf_op jit(solution)/shard_map/all_gather | solution.py:58
  11.1 5.2 %collective-permute-start = (bf16[2,256,256]{2,1,0:T(8,128)(2,1)}, bf16[2,256,256]{2,1,0:T(8,128)(2,1)}, u32[]{:S(2)}, u32[]{:S(2)}) collective-permute-start(bf16[2,256,256]{2,1,0:T(8,128)(2,1)} %bitcast.2), channel_id=1, source_target_pairs={{0,2},{1,3},{4,6},{5,7},{8,10},{9,11},{12,14},{13,15},{16,18},{17,... | collective-permute-start | bytes 786440 | tf_op jit(solution)/shard_map/ppermute | solution.py:22
  16.4 1.3 collective-permute-start.1
  17.7 0.9 dynamic-slice_bitcast_fusion
  18.6 0.7 fusion.38
  19.3 3.0 %bitcast_multiply_fusion.1 = bf16[2,128,3060]{1,0,2:T(2,128)(2,1)S(1)} fusion(bf16[1,2,128,3060]{2,1,3,0:T(2,128)(2,1)} %param.9, bf16[2,128]{1,0:T(2,128)(2,1)S(1)} %fusion.38), kind=kLoop, calls=%fused_computation.21 | loop fusion | flops 783360 | bytes 3133952 | tf_op jit(solution)/shard_map/mul | solution.py:86
  22.3 3.6 %fusion.13 = f32[2,3060,256]{2,1,0:T(8,128)} fusion(bf16[2,128,256]{2,1,0:T(8,128)(2,1)S(1)} %dynamic-slice_bitcast_fusion, bf16[2,128,3060]{1,0,2:T(2,128)(2,1)S(1)} %bitcast_multiply_fusion.1), kind=kOutput, calls=%fused_computation.19 | convolution fusion | flops 401080320 | bytes 7964672 | tf_op jit(solution)/shard_map/apn,apc->anc/dot_general | solution.py:92
  25.9 4.9 %reshape.185 = f32[2,9,340,256]{3,2,1,0:T(8,128)} reshape(f32[2,3060,256]{2,1,0:T(8,128)} %fusion.13) | data formatting | bytes 12533760 | tf_op jit(solution)/shard_map/reshape | solution.py:93
  30.7 5.1 %slice_bitcast_fusion.17 = (f32[340,256]{1,0:T(8,128)S(1)}, f32[340,256]{1,0:T(8,128)S(1)}, f32[340,256]{1,0:T(8,128)S(1)}, f32[340,256]{1,0:T(8,128)S(1)}, f32[...) fusion(f32[2,9,340,256]{3,2,1,0:T(8,128)} %reshape.185), kind=kLoop, calls=%fused_computation.49 | loop fusion | bytes 12533760 | tf_op jit(solution)/shard_map/mul | solution.py:100
  35.8 0.1 fusion.32
  35.9 5.2 %multiply_add_fusion = f32[6,340,256]{2,1,0:T(8,128)S(1)} fusion(f32[340,256]{1,0:T(8,128)S(1)} %get-tuple-element.15, f32[6]{0:T(128)S(1)} %get-tuple-element.37, f32[340,256]{1,0:T(8,128)S(1)} %get-tuple-element.16, f32[6]{0:T(128)S(1)} %get-tuple-element.38, f32[340,256]{1,0:T(8,128)S(1)} %get-tuple-element.17, f32[6]{0:T(128)S(1)} %get-tuple-element.39, ...), kind=kLoop, calls=%fused_computation.6 | loop fusion | flops 18278400 | bytes 8356272 | tf_op jit(solution)/shard_map/add | solution.py:101
  41.2 1.9 %broadcast_in_dim.27 = f32[6,8,2,8,2,256]{5,4,3,2,1,0:T(2,128)} broadcast(f32[6,8,8,256]{3,2,1,0:T(8,128)S(1)} %fusion.22), dimensions={0,1,3,5} | broadcast | bytes 1966080 | tf_op jit(solution)/shard_map/broadcast_in_dim | solution.py:48
  43.1 3.1 %reshape.186 = f32[6,256,256]{2,1,0:T(8,128)} reshape(f32[6,8,2,8,2,256]{5,4,3,2,1,0:T(2,128)} %broadcast_in_dim.27) | data formatting | bytes 3145728 | tf_op jit(solution)/shard_map/reshape | solution.py:49
  46.3 1.5 %broadcast_in_dim.29 = f32[6,4,4,4,4,256]{5,4,3,2,1,0:T(4,128)} broadcast(f32[6,4,4,256]{3,2,1,0:T(4,128)S(1)} %broadcast_in_dim.28), dimensions={0,1,3,5} | broadcast | bytes 1671168 | tf_op jit(solution)/shard_map/broadcast_in_dim | solution.py:48
  47.8 2.8 %reshape.187 = f32[6,256,256]{2,1,0:T(8,128)} reshape(f32[6,4,4,4,4,256]{5,4,3,2,1,0:T(4,128)} %broadcast_in_dim.29) | data formatting | bytes 3145728 | tf_op jit(solution)/shard_map/reshape | solution.py:49
  50.6 0.0 copy-start
  50.6 3.5 %fusion.40 = (bf16[6,256,256]{2,1,0:T(8,128)(2,1)S(1)}, f32[6,256,256]{2,1,0:T(8,128)}) fusion(f32[6,2,2,256]{3,2,1,0:T(2,128)S(1)} %broadcast_in_dim.60, f32[6,256,256]{2,1,0:T(8,128)} %reshape.187, f32[6,256,256]{2,1,0:T(8,128)} %reshape.186, f32[6,340,256]{2,1,0:T(8,128)S(1)} %multiply_add_fusion), kind=kLoop, calls=%fused_computation.136 | loop fusion | flops 1572864 | bytes 7102464 | tf_op jit(solution)/shard_map/convert.1
  54.2 1.3 collective-permute-start.4
  55.5 4.6 %collective-permute-start.5 = (bf16[2,256,256]{2,1,0:T(8,128)(2,1)S(1)}, bf16[2,256,256]{2,1,0:T(8,128)(2,1)S(1)}, u32[]{:S(2)}, u32[]{:S(2)}) collective-permute-start(bf16[2,256,256]{2,1,0:T(8,128)(2,1)S(1)} %get-tuple-element.35), channel_id=1, source_target_pairs={{0,4},{4,8},{8,12},{1,5},{5,9},{9,13},{2,6},{6,10},{10,14},{3,7},{... | collective-permute-start | bytes 786440 | tf_op jit(solution)/shard_map/ppermute | solution.py:22
  60.1 2.5 %fusion.46 = bf16[2,128,3060,1]{1,0,2,3:T(2,128)(2,1)} fusion(bf16[2,128]{1,0:T(2,128)(2,1)S(1)} %fusion.38, bf16[1,2,128,3060]{2,1,3,0:T(2,128)(2,1)S(1)} %copy-done), kind=kLoop, calls=%fused_computation.139 | loop fusion | flops 783360 | bytes 3133952 | tf_op jit(solution)/shard_map/mul | solution.py:86
  62.6 0.1 reshape.192
  62.7 0.6 fusion.43
  63.3 0.0 collective-permute-done
  63.3 0.0 collective-permute-done.1
  63.3 1.1 pad_maximum_fusion
  64.4 3.5 %collective-permute-start.2 = (bf16[2,2,256,256]{3,2,1,0:T(8,128)(2,1)S(1)}, bf16[2,2,256,256]{3,2,1,0:T(8,128)(2,1)S(1)}, u32[]{:S(2)}, u32[]{:S(2)}) collective-permute-start(bf16[2,2,256,256]{3,2,1,0:T(8,128)(2,1)S(1)} %pad_maximum_fusion), channel_id=1, source_target_pairs={{0,4},{4,8},{8,12},{1,5},{5,9},{9,13},{2,6},{6,10},{10,14},{3,7},{... | collective-permute-start | bytes 1572872 | tf_op jit(solution)/shard_map/ppermute | solution.py:22
  67.9 1.3 collective-permute-start.3
  69.2 0.0 collective-permute-done.4
  69.2 2.4 %multiply_convert_fusion.1 = (bf16[2,256,256]{2,1,0:T(8,128)(2,1)S(1)}, bf16[2,256,256]{2,1,0:T(8,128)(2,1)S(1)}) fusion(f32[]{:T(128)} %bitcast.56, bf16[2,256,256]{2,1,0:T(8,128)(2,1)S(1)} %collective-permute-done.5, f32[6,256,256]{2,1,0:T(8,128)} %get-tuple-element.11, bf16[2,256,256]{2,1,0:T(8,128)(2,1)S(1)} %collective-permute-done.4, f32[]{:T(128)} %bitcast.57), kind=kLoop, calls=%fused_computation.29 | loop fusion | flops 1048576 | bytes 1572872 | tf_op jit(solution)/shard_map/convert_element_type | solution.py:112
  71.7 5.3 %collective-permute-start.6 = (bf16[2,256,256]{2,1,0:T(8,128)(2,1)S(1)}, bf16[2,256,256]{2,1,0:T(8,128)(2,1)S(1)}, u32[]{:S(2)}, u32[]{:S(2)}) collective-permute-start(bf16[2,256,256]{2,1,0:T(8,128)(2,1)S(1)} %get-tuple-element.32), channel_id=1, source_target_pairs={{0,2},{1,3},{4,6},{5,7},{8,10},{9,11},{12,14},{13,15},{16,18},{17,... | collective-permute-start | bytes 786440 | tf_op jit(solution)/shard_map/ppermute | solution.py:22
  76.9 1.5 %collective-permute-start.7 = (bf16[2,256,256]{2,1,0:T(8,128)(2,1)S(1)}, bf16[2,256,256]{2,1,0:T(8,128)(2,1)S(1)}, u32[]{:S(2)}, u32[]{:S(2)}) collective-permute-start(bf16[2,256,256]{2,1,0:T(8,128)(2,1)S(1)} %get-tuple-element.33), channel_id=1, source_target_pairs={{2,0},{3,1},{6,4},{7,5},{10,8},{11,9},{14,12},{15,13},{18,16},{19,... | collective-permute-start | bytes 786440 | tf_op jit(solution)/shard_map/ppermute | solution.py:22
  78.5 3.1 %collective-permute-done.6 = bf16[2,256,256]{2,1,0:T(8,128)(2,1)S(1)} collective-permute-done((bf16[2,256,256]{2,1,0:T(8,128)(2,1)S(1)}, bf16[2,256,256]{2,1,0:T(8,128)(2,1)S(1)}, u32[]{:S(2)}, u32[]{:S(2)}) %collective-permute-start.6) | collective-permute-done | bytes 262176 | tf_op jit(solution)/shard_map/ppermute | solution.py:22
  81.6 4.1 %collective-permute-done.7 = bf16[2,256,256]{2,1,0:T(8,128)(2,1)S(1)} collective-permute-done((bf16[2,256,256]{2,1,0:T(8,128)(2,1)S(1)}, bf16[2,256,256]{2,1,0:T(8,128)(2,1)S(1)}, u32[]{:S(2)}, u32[]{:S(2)}) %collective-permute-start.7) | collective-permute-done | bytes 262176 | tf_op jit(solution)/shard_map/ppermute | solution.py:22
  85.7 0.1 convert_add_fusion
  85.8 0.0 collective-permute-done.2
  85.8 1.8 %multiply_bitcast_fusion = bf16[2,6,340,256]{3,2,1,0:T(8,128)(2,1)S(1)} fusion(bf16[2,2,256,256]{3,2,1,0:T(8,128)(2,1)S(1)} %collective-permute-done.3, bf16[1,2,256,256]{3,2,1,0:T(8,128)(2,1)} %bitcast.4, bf16[1,2,256,256]{3,2,1,0:T(8,128)(2,1)} %bitcast.3, bf16[2,2,256,256]{3,2,1,0:T(8,128)(2,1)S(1)} %collective-permute-done.2, ...), kind=kOutput, calls=%fused_computation.7 | convolution fusion | flops 539918336 | bytes 3835908 | tf_op jit(solution)/shard_map/mp,jwpc->jwmc/dot_general | solution.py:65
  87.6 4.7 %gather_fusion = bf16[18,2,340,256]{3,2,1,0:T(8,128)(2,1)} fusion(bf16[2,6,340,256]{3,2,1,0:T(8,128)(2,1)S(1)} %multiply_bitcast_fusion, s32[1024]{0:T(1024)S(1)} %pad_clamp_fusion), kind=kCustom, calls=%fused_computation | custom fusion | bytes 12533832 | tf_op jit(solution)/shard_map/gather | solution.py:78
  92.3 5.8 %copy.98 = bf16[2,9,2,340,256]{4,3,1,0,2:T(8,128)(2,1)} copy(bf16[2,9,2,340,256]{4,3,2,1,0:T(8,128)(2,1)} %bitcast.129) | data formatting | bytes 12533760 | tf_op jit(solution)/shard_map/gather | solution.py:78
  98.2 6.3 %reshape.189 = bf16[2,2,3060,256]{3,2,1,0:T(8,128)(2,1)} reshape(bf16[2,2,9,340,256]{4,3,2,1,0:T(8,128)(2,1)} %bitcast.131) | data formatting | bytes 12533760 | tf_op jit(solution)/shard_map/reshape | solution.py:87
  104.5 4.9 %fusion.16 = f32[2,256,128]{2,1,0:T(8,128)S(1)} fusion(bf16[2,128,3060,1]{1,0,2,3:T(2,128)(2,1)S(1)} %copy-done.2, bf16[2,2,3060,256]{3,2,1,0:T(8,128)(2,1)} %reshape.189), kind=kOutput, calls=%fused_computation.23 | convolution fusion | flops 802226176 | bytes 8095744 | tf_op jit(solution)/shard_map/apn,janc->japc/dot_general | solution.py:88
  109.3 0.1 copy.78
  109.5 0.1 fusion.23
  109.5 0.8 copy-done.1
  110.3 0.0 reduce-scatter.2.cloned.1.call-update
  110.4 4.6 %fusion.15 = bf16[9,340,2,128]{3,1,0,2:T(8,128)(2,1)S(1)} fusion(f32[2,128]{1,0:T(2,128)S(1)} %convert_multiply_fusion, bf16[2,2,9,340,256]{4,3,0,2,1:T(8,128)(2,1)} %bitcast.130, bf16[2,128,256]{2,1,0:T(8,128)(2,1)S(1)} %copy-done.4), kind=kOutput, calls=%fused_computation.22 | convolution fusion | flops 803727360 | bytes 7965696 | tf_op jit(solution)/shard_map/jakmc,japc->kmap/dot_general | solution.py:80
  115.1 0.3 convert_element_type.70
  115.4 12.1 %copy.79 = bf16[1,2,128,3060]{2,1,3,0:T(2,128)(2,1)} copy(bf16[1,2,128,3060]{2,3,1,0:T(8,128)(2,1)S(1)} %bitcast.132) | data formatting | bytes 3133440
  (35 shorter events, 0.3 us)
Async XLA Ops:
  7.2 120.3 %reduce-scatter.2.cloned.1.call-start = ((), (), s32[]{:S(2)}) async-start(), calls=%async_computation.1 | async-start | bytes 786432 | tf_op jit(solution)/shard_map/reduce_scatter | solution.py:117
  11.1 52.2 %collective-permute-start = (bf16[2,256,256]{2,1,0:T(8,128)(2,1)}, bf16[2,256,256]{2,1,0:T(8,128)(2,1)}, u32[]{:S(2)}, u32[]{:S(2)}) collective-permute-start(bf16[2,256,256]{2,1,0:T(8,128)(2,1)} %bitcast.2), channel_id=1, source_target_pairs={{0,2},{1,3},{4,6},{5,7},{8,10},{9,11},{12,14},{13,15},{16,18},{17,... | collective-permute-start | bytes 786440 | tf_op jit(solution)/shard_map/ppermute | solution.py:22
  16.4 46.9 %collective-permute-start.1 = (bf16[2,256,256]{2,1,0:T(8,128)(2,1)}, bf16[2,256,256]{2,1,0:T(8,128)(2,1)}, u32[]{:S(2)}, u32[]{:S(2)}) collective-permute-start(bf16[2,256,256]{2,1,0:T(8,128)(2,1)} %bitcast.2), channel_id=1, source_target_pairs={{2,0},{3,1},{6,4},{7,5},{10,8},{11,9},{14,12},{15,13},{18,16},{19,... | collective-permute-start | bytes 786440 | tf_op jit(solution)/shard_map/ppermute | solution.py:22
  18.6 3.7 %copy-start.3 = (bf16[2,128,256]{2,1,0:T(8,128)(2,1)}, bf16[2,128,256]{2,1,0:T(8,128)(2,1)S(1)}, u32[]{:S(2)}) copy-start(bf16[2,128,256]{2,1,0:T(8,128)(2,1)S(1)} %dynamic-slice_bitcast_fusion) | copy-start | bytes 393220
  30.7 5.1 %copy-start.6 = (s32[2,9]{1,0:T(2,128)S(1)}, s32[2,9]{1,0:T(2,128)}, u32[]{:S(2)}) copy-start(s32[2,9]{1,0:T(2,128)} %param.6) | copy-start | bytes 220
  50.6 9.4 %copy-start = (bf16[1,2,128,3060]{2,1,3,0:T(2,128)(2,1)S(1)}, bf16[1,2,128,3060]{2,1,3,0:T(2,128)(2,1)}, u32[]{:S(2)}) copy-start(bf16[1,2,128,3060]{2,1,3,0:T(2,128)(2,1)} %param.9) | copy-start | bytes 4700164
  54.1 8.5 %copy-start.7 = (s32[1,2]{1,0:T(1,128)S(1)}, s32[1,2]{1,0:T(1,128)}, u32[]{:S(2)}) copy-start(s32[1,2]{1,0:T(1,128)} %param.7) | copy-start | bytes 28
  54.2 15.0 %collective-permute-start.4 = (bf16[2,256,256]{2,1,0:T(8,128)(2,1)S(1)}, bf16[2,256,256]{2,1,0:T(8,128)(2,1)S(1)}, u32[]{:S(2)}, u32[]{:S(2)}) collective-permute-start(bf16[2,256,256]{2,1,0:T(8,128)(2,1)S(1)} %get-tuple-element.34), channel_id=1, source_target_pairs={{4,0},{8,4},{12,8},{5,1},{9,5},{13,9},{6,2},{10,6},{14,10},{7,3},{... | collective-permute-start | bytes 786440 | tf_op jit(solution)/shard_map/ppermute | solution.py:22
  55.5 13.8 %collective-permute-start.5 = (bf16[2,256,256]{2,1,0:T(8,128)(2,1)S(1)}, bf16[2,256,256]{2,1,0:T(8,128)(2,1)S(1)}, u32[]{:S(2)}, u32[]{:S(2)}) collective-permute-start(bf16[2,256,256]{2,1,0:T(8,128)(2,1)S(1)} %get-tuple-element.35), channel_id=1, source_target_pairs={{0,4},{4,8},{8,12},{1,5},{5,9},{9,13},{2,6},{6,10},{10,14},{3,7},{... | collective-permute-start | bytes 786440 | tf_op jit(solution)/shard_map/ppermute | solution.py:22
  64.4 21.4 %collective-permute-start.2 = (bf16[2,2,256,256]{3,2,1,0:T(8,128)(2,1)S(1)}, bf16[2,2,256,256]{3,2,1,0:T(8,128)(2,1)S(1)}, u32[]{:S(2)}, u32[]{:S(2)}) collective-permute-start(bf16[2,2,256,256]{3,2,1,0:T(8,128)(2,1)S(1)} %pad_maximum_fusion), channel_id=1, source_target_pairs={{0,4},{4,8},{8,12},{1,5},{5,9},{9,13},{2,6},{6,10},{10,14},{3,7},{... | collective-permute-start | bytes 1572872 | tf_op jit(solution)/shard_map/ppermute | solution.py:22
  67.9 17.9 %collective-permute-start.3 = (bf16[2,2,256,256]{3,2,1,0:T(8,128)(2,1)S(1)}, bf16[2,2,256,256]{3,2,1,0:T(8,128)(2,1)S(1)}, u32[]{:S(2)}, u32[]{:S(2)}) collective-permute-start(bf16[2,2,256,256]{3,2,1,0:T(8,128)(2,1)S(1)} %pad_maximum_fusion), channel_id=1, source_target_pairs={{4,0},{8,4},{12,8},{5,1},{9,5},{13,9},{6,2},{10,6},{14,10},{7,3},{... | collective-permute-start | bytes 1572872 | tf_op jit(solution)/shard_map/ppermute | solution.py:22
  71.7 9.9 %collective-permute-start.6 = (bf16[2,256,256]{2,1,0:T(8,128)(2,1)S(1)}, bf16[2,256,256]{2,1,0:T(8,128)(2,1)S(1)}, u32[]{:S(2)}, u32[]{:S(2)}) collective-permute-start(bf16[2,256,256]{2,1,0:T(8,128)(2,1)S(1)} %get-tuple-element.32), channel_id=1, source_target_pairs={{0,2},{1,3},{4,6},{5,7},{8,10},{9,11},{12,14},{13,15},{16,18},{17,... | collective-permute-start | bytes 786440 | tf_op jit(solution)/shard_map/ppermute | solution.py:22
  76.9 8.8 %collective-permute-start.7 = (bf16[2,256,256]{2,1,0:T(8,128)(2,1)S(1)}, bf16[2,256,256]{2,1,0:T(8,128)(2,1)S(1)}, u32[]{:S(2)}, u32[]{:S(2)}) collective-permute-start(bf16[2,256,256]{2,1,0:T(8,128)(2,1)S(1)} %get-tuple-element.33), channel_id=1, source_target_pairs={{2,0},{3,1},{6,4},{7,5},{10,8},{11,9},{14,12},{15,13},{18,16},{19,... | collective-permute-start | bytes 786440 | tf_op jit(solution)/shard_map/ppermute | solution.py:22
  98.2 6.3 %copy-start.2 = (bf16[2,128,3060,1]{1,0,2,3:T(2,128)(2,1)S(1)}, bf16[2,128,3060,1]{1,0,2,3:T(2,128)(2,1)}, u32[]{:S(2)}) copy-start(bf16[2,128,3060,1]{1,0,2,3:T(2,128)(2,1)} %fusion.46) | copy-start | bytes 4700164
  104.4 5.9 %copy-start.5 = (s32[2,256]{1,0:T(2,128)S(1)}, s32[2,256]{1,0:T(2,128)}, u32[]{:S(2)}) copy-start(s32[2,256]{1,0:T(2,128)} %param.8) | copy-start | bytes 6148
  104.4 5.9 %copy-start.4 = (bf16[2,128,256]{2,1,0:T(8,128)(2,1)S(1)}, bf16[2,128,256]{2,1,0:T(8,128)(2,1)}, u32[]{:S(2)}) copy-start(bf16[2,128,256]{2,1,0:T(8,128)(2,1)} %copy-done.3) | copy-start | bytes 393220
  109.5 0.8 copy-start.1
Sparse Core Ops, SparseCore 0:
  110.5 7.9 reduce-scatter.1
